TPU v7x, 512 devices: a whole 4x8x8 slice. The times are simulated.
512 devices in a mesh: dp: 32 (over x, z), tensor: 16 (over y, core).
Axes of the slice: x: 4, y: 8, z: 8, core: 2. Of those that a mesh axis runs over, the one named last changes fastest.
Arguments:
- activations: bfloat16 [16384, 16384], P('dp', 'tensor'), may hold values from -40 to 40, as said below
- token_ids: int32 [16384], P('dp'), may hold values from 0 to 128004, as said below
- weight: bfloat16 [16384, 16384], P('dp', 'tensor'), may hold values from -6 to 6
- inv_chol: float32 [128, 128, 1024], P('tensor', 'dp'), may hold values from -1 to 2, as said below
- bit_widths: int32 [128], P('tensor'), may hold values from 2 to 8, as said below
Outputs:
- quantized: bfloat16 [16384, 16384], P('dp', 'tensor')
- gram_blocks: float32 [128, 128, 128], P('tensor', 'dp')
- block_errors: float32 [128, 4], replicated
Inputs may be any that keep to these rules, and one draw needn't show every extreme that they name: `token_ids`: id 128004 marks padding. In the d-th aligned block of 512 tokens (d = 0 .. 31), exactly 170 + d*342//31 tokens are not padding, at positions drawn from the seed; the last block has no padding. `bit_widths`: each entry is 2, 3, 4 or 8. `inv_chol`: row i of block b, with j = b mod (8), holds a positive entry at column j*128+i, arbitrary entries at columns from (j+1)*128 on, and zeros elsewhere. `activations`: finite values.
All inputs are finite; a program needn't handle non-finite values.
Results may differ from a plain program's by a relative error of at most 0.001.
Values sent between devices are 32-bit elements; how exact they have to be, the bound alone decides.
No kernel may reach another device: no remote copies, remote signals or barrier semaphores. Data moves between devices by JAX's collectives and lax.ppermute only.
A program may use at most 64 MiB of HBM per device.

v0:
```python
import jax
import jax.numpy as jnp
from jax import lax
from jax.sharding import PartitionSpec as P

OUT = 16384
BLK = 128
PANEL = 1024


pad_token = 128004


def level_count(widths):
    return jnp.where(
        widths == 2, 2.0, jnp.where(widths == 3, 4.0, jnp.where(widths == 4, 8.0, 128.0))
    ).astype(jnp.float32)


def soft_quantize(values, levels):
    largest = jnp.max(jnp.abs(values), axis=-1, keepdims=True)
    step_size = (largest + 1e-06) / (levels - 0.5)
    scaled = values / step_size
    smooth = scaled - jnp.sin(2.0 * jnp.pi * scaled) / (2.0 * jnp.pi)
    return step_size * jnp.clip(smooth, -levels, levels - 1.0)


def per_device(activations, token_ids, weight, inv_chol, bit_widths):
    token_count, width = activations.shape
    row_count = weight.shape[0]
    blocks_here = width // BLK
    panels_here = width // PANEL
    per_panel = PANEL // BLK
    live = token_ids != pad_token
    live_local = jnp.sum(live.astype(jnp.float32))
    masked = activations * live.astype(activations.dtype)[:, None]
    partial_gram = jnp.einsum(
        "tbi,tbj->bij",
        masked.reshape(token_count, blocks_here, BLK),
        activations.reshape(token_count, blocks_here, BLK),
        preferred_element_type=jnp.float32,
    )
    gram_sum, count = lax.psum((partial_gram, live_local), "dp")
    gram = gram_sum / count
    owned_rows = BLK // lax.axis_size("dp")
    gram_out = lax.dynamic_slice_in_dim(gram, lax.axis_index("dp") * owned_rows, owned_rows, 1)
    initial = weight.astype(jnp.float32).reshape(row_count, blocks_here, BLK)
    error_terms = []
    for levels in (2.0, 4.0, 8.0, 128.0):
        delta = initial - soft_quantize(initial, levels)
        weighted = jnp.einsum("rbi,bij->rbj", delta, gram, precision=lax.Precision.HIGHEST)
        error_terms.append(jnp.sum(weighted * delta, axis=(0, 2)) * (levels * levels / (OUT * BLK)))
    partial_errors = jnp.stack(error_terms, axis=1)
    summed_rows = lax.psum(partial_errors, "dp")
    block_errors = lax.all_gather(summed_rows, "tensor", axis=0, tiled=True)
    level_panels = level_count(bit_widths).reshape(panels_here, per_panel)
    factor_whole = lax.all_gather(inv_chol, "dp", axis=1, tiled=True).reshape(
        panels_here, per_panel, BLK, PANEL
    )
    current = weight.astype(jnp.float32).reshape(row_count, panels_here, PANEL)
    outputs = []
    for column_block in range(per_panel):
        first_column = column_block * BLK
        block_values = current[:, :, first_column : first_column + BLK]
        block_levels = level_panels[:, column_block][None, :, None]
        quantized_block = soft_quantize(block_values, block_levels)
        outputs.append(quantized_block.astype(jnp.bfloat16))
        if column_block + 1 < per_panel:
            factor_block = factor_whole[:, column_block, :, first_column:]
            diagonal = jnp.diagonal(factor_block[:, :, :BLK], axis1=1, axis2=2)
            scaled_error = (block_values - quantized_block) / diagonal[None, :, :]
            update = jnp.einsum(
                "rpi,pij->rpj",
                scaled_error,
                factor_block[:, :, BLK:],
                precision=lax.Precision.HIGHEST,
            )
            current = jnp.concatenate(
                [current[:, :, : first_column + BLK], current[:, :, first_column + BLK :] - update],
                axis=2,
            )
    quantized = jnp.concatenate(outputs, axis=2).reshape(row_count, width)
    return (quantized, gram_out, block_errors)


def solution(mesh):
    placed = (P("dp", "tensor"), P("dp"), P("dp", "tensor"), P("tensor", "dp", None), P("tensor"))
    return jax.shard_map(
        per_device,
        mesh=mesh,
        in_specs=placed,
        out_specs=(P("dp", "tensor"), P("tensor", "dp", None), P()),
        check_vma=False,
    )
```

profile of v0, /device:TPU:1, one launch (start us, length us, event | category | flops | bytes accessed | tf_op | source)
XLA Modules:
  0.0 405.2 jit_solution(1819908722294077211)
XLA Ops:
  7.2 1.3 convert_reduce_fusion
  8.5 1.4 broadcast_multiply_fusion
  10.6 1.3 fusion.9
  12.7 68.5 %psum.22 = f32[]{:T(128)} all-reduce(f32[]{:T(128)} %get-tuple-element.3), channel_id=1, replica_groups=mesh['dp'=32,'tensor'=16] {'dp'}, use_global_device_ids=true, to_apply=%region_10.11 | all-reduce | flops 1 | bytes 8 | tf_op jit(solution)/shard_map/psum | solution.py:43
  97.1 1.6 convert_bitcast_fusion
  99.1 1.9 copy.92
  102.9 2.0 convert_dynamic-update-slice_fusion.6
  104.8 68.8 %all-reduce.2.cloned.1.call-done = f32[8,128,128]{2,1,0:T(8,128)} async-done(((f32[8,128,128]{2,1,0:T(8,128)}), f32[8,128,128]{2,1,0:T(8,128)}) %all-reduce.2.cloned.1.call-update) | async-done | bytes 524304 | tf_op jit(solution)/shard_map/psum | solution.py:43
  173.6 1.8 broadcast_divide_fusion
  175.4 18.9 %fusion.3 = f32[8]{0:T(128)S(1)} fusion(f32[8,128,128]{2,1,0:T(8,128)S(1)} %broadcast_divide_fusion, f32[512,8,128]{0,2,1:T(8,128)} %copy.92, f32[512,8]{0,1:T(8,128)S(1)} %get-tuple-element.7), kind=kOutput, calls=%fused_computation.17 | convolution fusion | flops 813694976 | bytes 2637856 | tf_op jit(solution)/shard_map/rbi,bij->rbj/dot_general | solution.py:51
  194.3 18.9 %fusion.2 = f32[8]{0:T(128)S(1)} fusion(f32[8,128,128]{2,1,0:T(8,128)S(1)} %broadcast_divide_fusion, f32[512,8,128]{0,2,1:T(8,128)S(1)} %copy-done.1, f32[512,8]{0,1:T(8,128)S(1)} %get-tuple-element.8), kind=kOutput, calls=%fused_computation.15 | convolution fusion | flops 813694976 | bytes 2637856 | tf_op jit(solution)/shard_map/rbi,bij->rbj/dot_general | solution.py:51
  213.3 18.9 %fusion.1 = f32[8]{0:T(128)S(1)} fusion(f32[8,128,128]{2,1,0:T(8,128)S(1)} %broadcast_divide_fusion, f32[512,8,128]{0,2,1:T(8,128)S(1)} %copy-done.1, f32[512,8]{0,1:T(8,128)S(1)} %get-tuple-element.9), kind=kOutput, calls=%fused_computation.13 | convolution fusion | flops 813694976 | bytes 2637856 | tf_op jit(solution)/shard_map/rbi,bij->rbj/dot_general | solution.py:51
  232.2 18.9 %fusion = f32[8]{0:T(128)S(1)} fusion(f32[8,128,128]{2,1,0:T(8,128)S(1)} %broadcast_divide_fusion, f32[512,8,128]{0,2,1:T(8,128)S(1)} %copy-done.1, f32[512,8]{0,1:T(8,128)S(1)} %get-tuple-element.10), kind=kOutput, calls=%fused_computation.11 | convolution fusion | flops 813694976 | bytes 2637856 | tf_op jit(solution)/shard_map/rbi,bij->rbj/dot_general | solution.py:51
  251.1 58.3 %psum.23 = f32[8,4]{0,1:T(4,128)S(1)} all-reduce(f32[8,4]{0,1:T(4,128)S(1)} %pad_maximum_fusion), channel_id=1, replica_groups=mesh['dp'=32,'tensor'=16] {'dp'}, use_global_device_ids=true, to_apply=%region_16.17 | all-reduce | flops 32 | bytes 256 | tf_op jit(solution)/shard_map/psum | solution.py:54
  309.4 48.2 %all-gather = f32[16,8,4]{1,2,0:T(4,128)S(1)} all-gather(f32[1,8,4]{1,2,0:T(4,128)S(1)} %bitcast.214), channel_id=1, replica_groups=mesh['dp'=32,'tensor'=16] {'tensor'}, dimensions={0}, use_global_device_ids=true | all-gather | bytes 2176 | tf_op jit(solution)/shard_map/all_gather | solution.py:55
  358.9 4.6 %copy.128 = f32[8,128,1024]{2,1,0:T(8,128)S(1)} copy(f32[8,128,1024]{2,0,1:T(8,128)} %all-gather.3.cloned.1.call-done) | data formatting | bytes 8388608 | tf_op jit(solution)/shard_map/all_gather | solution.py:57
  363.8 1.2 gather_fusion.6
  365.0 1.2 gather_fusion.5
  366.3 1.2 gather_fusion.4
  367.6 1.2 gather_fusion.3
  368.8 1.2 gather_fusion.2
  370.1 1.2 gather_fusion
  371.4 1.2 gather_fusion.1
  372.6 4.1 %slice_subtract_fusion = f32[512,1,896]{2,0,1:T(8,128)S(1)} fusion(f32[512,1,1024]{2,0,1:T(8,128)} %get-tuple-element.6, f32[1,128,1024]{2,1,0:T(8,128)S(1)} %slice_bitcast_fusion, f32[128]{0:T(128)S(1)} %gather_fusion, f32[]{:T(128)} %bitcast.4, f32[]{:T(128)} %bitcast.3, f32[512]{0:T(512)S(1)} %add_divide_fusion.7), kind=kOutput, calls=%fused_computation.23 | convolution fusion | flops 705691648 | bytes 4393480 | tf_op jit(solution)/shard_map/rpi,pij->rpj/dot_general | solution.py:72
  378.1 2.4 slice_subtract_fusion.1
  381.7 2.1 fusion.4
  385.1 2.0 fusion.5
  388.5 1.8 fusion.6
  390.5 1.1 convert_dynamic-update-slice_fusion.1
  391.6 1.5 fusion.7
  394.4 1.4 abs_reduce_fusion.1
  395.9 1.1 fusion.60
  (67 shorter events, 13.6 us)
Async XLA Ops:
  7.2 166.5 %all-reduce.2.cloned.1.call-start = ((), (), s32[]{:S(2)}) async-start(), calls=%async_computation.1 | async-start | bytes 1048576 | tf_op jit(solution)/shard_map/psum | solution.py:43
  8.5 2.0 copy-start
  10.5 1.4 copy-start.3
  10.5 70.6 %copy-start.5 = (s32[8]{0:T(128)S(1)}, s32[8]{0:T(128)}, u32[]{:S(2)}) copy-start(s32[8]{0:T(128)} %param.9) | copy-start | bytes 100
  10.5 86.5 %copy-start.2 = (bf16[512,1024]{1,0:T(8,128)(2,1)S(1)}, bf16[512,1024]{1,0:T(8,128)(2,1)}, u32[]{:S(2)}) copy-start(bf16[512,1024]{1,0:T(8,128)(2,1)} %param.7) | copy-start | bytes 3145732
  11.8 347.1 %all-gather.3.cloned.1.call-start = ((), (), s32[]{:S(2)}) async-start(), calls=%async_computation | async-start | bytes 4325376 | tf_op jit(solution)/shard_map/all_gather | solution.py:57
  175.4 18.9 %copy-start.1 = (f32[512,8,128]{0,2,1:T(8,128)S(1)}, f32[512,8,128]{0,2,1:T(8,128)}, u32[]{:S(2)}) copy-start(f32[512,8,128]{0,2,1:T(8,128)} %copy.92) | copy-start | bytes 6291460
  397.0 1.0 copy-start.4
Sparse Core Ops, SparseCore 0:
  12.0 161.6 all-reduce.1
  176.8 85.7 all-gather.2
where the time goes:
time: 413 us; the launch traced here: 405 us
  blocking collectives  175 us (42%)
  matrix products  92.2 us (22%)
  waiting for transfers between devices  68.8 us (17%)
  between operations  30 us (7%)
  local copies, waits for them, and re-layouts  20.2 us (5%)
  other arithmetic  18.7 us (5%)
    dot_general x4, matrix products, per_device(): jnp.einsum('rbi,bij->rbj', delta, gram, precision=lax.Precision.HIGHEST)  75.6 us
    psum x1, waiting for transfers between devices, per_device(): gram_sum, count = lax.psum((partial_gram, live_local), 'dp')  68.8 us
    psum x1, blocking collectives, per_device(): gram_sum, count = lax.psum((partial_gram, live_local), 'dp')  68.5 us
    psum x1, blocking collectives, per_device(): summed_rows = lax.psum(partial_errors, 'dp')  58.3 us
    all_gather x1, blocking collectives, per_device(): block_errors = lax.all_gather(summed_rows, 'tensor', axis=0, tiled=True)  48.2 us
    dot_general x7, matrix products, per_device(): jnp.einsum('rpi,pij->rpj', scaled_error, factor_block[:, :, BLK:], precis...  15.4 us
    unnamed x8, other arithmetic  10.2 us
    gather x7, local copies, waits for them, and re-layouts, per_device(): diagonal = jnp.diagonal(factor_block[:, :, :BLK], axis1=1, axis2=2)  8.72 us
  transfers between devices with their start and end apart: 2, of which 1 were waited for; matrix products, arithmetic and copies ran while one was open for 22% of the time, Pallas kernels for 0%

commit v1 on v0

v1 whole, which is shorter than its diff:
```python
import jax
import jax.numpy as jnp
from jax import lax
from jax.experimental import pallas as pl
from jax.experimental.pallas import tpu as pltpu
from jax.sharding import Mesh, PartitionSpec as P

OUT = 16384
BLK = 128
PANEL = 1024
NB = 8
DP = 32
ROWS = BLK // DP
NX, NZ, NY, NC = 4, 8, 8, 2
PAIRS = [(j, c) for j in range(NB) for c in range(j + 1, NB)]
NP = len(PAIRS) + 1
PAD = 128004
LEVELS = (2.0, 4.0, 8.0, 128.0)

SIN = (
    0.9999996039231652,
    -6.579691570100355,
    12.986436001995736,
    -12.188101551479916,
    6.558042314696102,
    -1.9530321174789678,
)


def sine_over_two_pi(u):
    r = u - jnp.round(u)
    z = r * r
    p = SIN[-1] * z + SIN[-2]
    for a in SIN[-3::-1]:
        p = p * z + a
    return p * r


def params(*semantics):
    return pltpu.CompilerParams(dimension_semantics=semantics, vmem_limit_bytes=56 << 20)


def pack_kernel(first_ref, f_ref, o_ref):
    lane = lax.broadcasted_iota(jnp.int32, (ROWS, BLK), 1)
    row = lax.broadcasted_iota(jnp.int32, (ROWS, BLK), 0)
    on_diag = lane == row + first_ref[0]
    diag = jnp.zeros((ROWS, BLK), jnp.float32)
    for j in range(NB):
        tile = f_ref[j, :, j * BLK : (j + 1) * BLK]
        value = jnp.sum(jnp.where(on_diag, tile, 0.0), axis=1, keepdims=True)
        diag = jnp.where(lane == j, value, diag)
    for i in range(NZ):
        for p, (j, c) in enumerate(PAIRS):
            o_ref[i, p] = f_ref[j, :, c * BLK : (c + 1) * BLK]
        o_ref[i, NP - 1] = diag


def pack_factor(first, factor):
    return pl.pallas_call(
        pack_kernel,
        out_shape=jax.ShapeDtypeStruct((NZ, NP, ROWS, BLK), jnp.float32),
        in_specs=[
            pl.BlockSpec(memory_space=pltpu.SMEM),
            pl.BlockSpec(memory_space=pltpu.VMEM),
        ],
        out_specs=pl.BlockSpec(memory_space=pltpu.VMEM),
        compiler_params=params(),
        name="pack_factor",
    )(first, factor)


def gram_kernel(tok_ref, a_ref, o_ref):
    live = jnp.where(tok_ref[...] != PAD, 1.0, 0.0).astype(jnp.bfloat16)
    x = a_ref[...]
    g = jnp.dot(x.T * live, x, preferred_element_type=jnp.float32)
    for d in range(DP):
        o_ref[d, 0] = g[d * ROWS : (d + 1) * ROWS]


def gram_partial(tokens, activations):
    n = activations.shape[0]
    return pl.pallas_call(
        gram_kernel,
        out_shape=jax.ShapeDtypeStruct((DP, NB, ROWS, BLK), jnp.float32),
        grid=(NB,),
        in_specs=[
            pl.BlockSpec((1, n), lambda b: (0, 0)),
            pl.BlockSpec((n, BLK), lambda b: (0, b)),
        ],
        out_specs=pl.BlockSpec((DP, 1, ROWS, BLK), lambda b: (0, b, 0, 0)),
        compiler_params=params("arbitrary"),
        name="gram_partial",
    )(tokens, activations)


def sum_kernel(g_ref, own_ref, o_ref):
    total = g_ref[0]
    for d in range(1, DP):
        total = total + g_ref[d]
    own_ref[...] = total
    for d in range(DP):
        o_ref[d] = total


def sum_rows(received):
    return pl.pallas_call(
        sum_kernel,
        out_shape=(
            jax.ShapeDtypeStruct((NB, ROWS, BLK), jnp.float32),
            jax.ShapeDtypeStruct((DP, NB, ROWS, BLK), jnp.float32),
        ),
        in_specs=[pl.BlockSpec(memory_space=pltpu.VMEM)],
        out_specs=(pl.BlockSpec(memory_space=pltpu.VMEM),) * 2,
        compiler_params=params(),
        name="sum_rows",
    )(received)


def error_kernel(w_ref, o_ref):
    w = w_ref[...].astype(jnp.float32)
    bound = jnp.max(jnp.abs(w), axis=1, keepdims=True) + 1e-6
    unit = w * (1.0 / bound)
    for k, levels in enumerate(LEVELS):
        u = unit * (levels - 0.5)
        smooth = jnp.clip(u - sine_over_two_pi(u), -levels, levels - 1.0)
        e = (w - (bound * (1.0 / (levels - 0.5))) * smooth).astype(jnp.bfloat16)
        s = lax.dot_general(e, e, (((0,), (0,)), ((), ())), preferred_element_type=jnp.float32)
        for d in range(DP):
            o_ref[0, k, d] = s[d * ROWS : (d + 1) * ROWS]


def error_grams(weight):
    rows = weight.shape[0]
    return pl.pallas_call(
        error_kernel,
        out_shape=jax.ShapeDtypeStruct((NB, 4, DP, ROWS, BLK), jnp.float32),
        grid=(NB,),
        in_specs=[pl.BlockSpec((rows, BLK), lambda b: (0, b))],
        out_specs=pl.BlockSpec((1, 4, DP, ROWS, BLK), lambda b: (b, 0, 0, 0, 0)),
        compiler_params=params("arbitrary"),
        name="error_grams",
    )(weight)


def score_kernel(tok_ref, g_ref, s_ref, o_ref):
    b = pl.program_id(0)
    lane = lax.broadcasted_iota(jnp.int32, (1, BLK), 1)

    @pl.when(b == 0)
    def _():
        live = jnp.sum(jnp.where(tok_ref[...] != PAD, 1.0, 0.0))
        o_ref[...] = jnp.where(lane == 4 * NB, live, 0.0)

    row = o_ref[...]
    for k in range(4):
        acc = g_ref[0, 0] * s_ref[0, k, 0]
        for d in range(1, DP):
            acc = acc + g_ref[d, 0] * s_ref[0, k, d]
        row = jnp.where(lane == 4 * b + k, jnp.sum(acc), row)
    o_ref[...] = row


def scores(tokens, gram, grams):
    n = tokens.shape[1]
    return pl.pallas_call(
        score_kernel,
        out_shape=jax.ShapeDtypeStruct((1, BLK), jnp.float32),
        grid=(NB,),
        in_specs=[
            pl.BlockSpec((1, n), lambda b: (0, 0)),
            pl.BlockSpec((DP, 1, ROWS, BLK), lambda b: (0, b, 0, 0)),
            pl.BlockSpec((1, 4, DP, ROWS, BLK), lambda b: (b, 0, 0, 0, 0)),
        ],
        out_specs=pl.BlockSpec((1, BLK), lambda b: (0, 0)),
        compiler_params=params("arbitrary"),
        name="scores",
    )(tokens, gram, grams)


CHUNKS = 2


def quant_kernel(bits_ref, x_ref, w_ref, own_ref, left_ref, right_ref, far0_ref, far1_ref, o_ref, c_ref, u_ref, slab_ref):
    rows = w_ref.shape[0] // CHUNKS
    x = x_ref[0]

    def slab(p):
        for off, refs in ((0, (own_ref,)), (NX - 1, (left_ref,)), (1, (right_ref,)), (2, (far0_ref, far1_ref))):
            base = pl.multiple_of(lax.rem(x + off, NX) * (NZ * ROWS), NZ * ROWS)
            chunk = jnp.concatenate([ref[i, p] for ref in refs for i in range(ref.shape[0])], axis=0)
            slab_ref[pl.ds(base, NZ * ROWS), :] = chunk
        return slab_ref[...]

    inv_diag = 1.0 / slab(NP - 1)[:, :NB].T
    p = 0
    for j in range(NB):
        first = j * BLK
        width = PANEL - first - BLK
        if width:
            for i in range(width // BLK):
                u = slab(p)
                p += 1
                high = u.astype(jnp.bfloat16)
                low = (u - high.astype(jnp.float32)).astype(jnp.bfloat16)
                cols = slice(i * BLK, (i + 1) * BLK)
                u_ref[0:BLK, cols] = high
                u_ref[BLK : 2 * BLK, cols] = high
                u_ref[2 * BLK : 3 * BLK, cols] = low
        bits = bits_ref[j]
        levels = jnp.where(bits == 2, 2.0, jnp.where(bits == 3, 4.0, jnp.where(bits == 4, 8.0, 128.0)))
        half = levels - 0.5
        for h in range(CHUNKS):
            part = slice(h * rows, (h + 1) * rows)
            if j == 0:
                c = w_ref[part, :BLK].astype(jnp.float32)
            else:
                c = c_ref[part, first : first + BLK]
            step = (jnp.max(jnp.abs(c), axis=1, keepdims=True) + 1e-6) / half
            u = c * (1.0 / step)
            q = step * jnp.clip(u - sine_over_two_pi(u), -levels, levels - 1.0)
            o_ref[part, first : first + BLK] = q.astype(jnp.bfloat16)
            if width:
                e = (c - q) * inv_diag[j : j + 1, :]
                high = e.astype(jnp.bfloat16)
                low = (e - high.astype(jnp.float32)).astype(jnp.bfloat16)
                lhs = jnp.concatenate([high, low, high], axis=1)
                update = jnp.dot(lhs, u_ref[:, :width], preferred_element_type=jnp.float32)
                if j == 0:
                    rest = w_ref[part, BLK:].astype(jnp.float32)
                else:
                    rest = c_ref[part, first + BLK :]
                c_ref[part, first + BLK :] = rest - update


def quantize(bits, x, weight, factor):
    rows = weight.shape[0]
    return pl.pallas_call(
        quant_kernel,
        out_shape=jax.ShapeDtypeStruct((rows, PANEL), jnp.bfloat16),
        in_specs=[
            pl.BlockSpec(memory_space=pltpu.SMEM),
            pl.BlockSpec(memory_space=pltpu.SMEM),
        ]
        + [pl.BlockSpec(memory_space=pltpu.VMEM)] * 6,
        out_specs=pl.BlockSpec(memory_space=pltpu.VMEM),
        scratch_shapes=[
            pltpu.VMEM((rows, PANEL), jnp.float32),
            pltpu.VMEM((3 * BLK, PANEL - BLK), jnp.bfloat16),
            pltpu.VMEM((BLK, BLK), jnp.float32),
        ],
        compiler_params=params(),
        name="quantize",
    )(bits, x, weight, *factor)


def exchange(pieces, axes):
    return lax.all_to_all(pieces, axes, 0, 0, tiled=False)


def to_all(piece, axes, count):
    return exchange(jnp.broadcast_to(piece[None], (count,) + piece.shape), axes)


def shift_x(piece, by):
    return lax.ppermute(piece, "x", [(i, (i + by) % NX) for i in range(NX)])


def per_device(activations, token_ids, weight, inv_chol, bit_widths):
    dp = ("x", "z")
    tensor = ("y", "c")
    half = NZ // 2
    tokens = token_ids.reshape(1, -1)
    x = lax.axis_index("x").reshape(1).astype(jnp.int32)
    first = (lax.axis_index(dp) * ROWS).reshape(1).astype(jnp.int32)
    packed = pack_factor(first, inv_chol)
    over_z = exchange(packed, "z")
    partial = gram_partial(tokens, activations)
    grams = error_grams(weight)
    over_z, partial = lax.optimization_barrier((over_z, partial))
    gram_rows = exchange(partial, dp)
    left = shift_x(over_z, 1)
    right = shift_x(over_z, -1)
    far0 = shift_x(left[:half], 1)
    far1 = shift_x(right[half:], -1)
    own, copies = sum_rows(gram_rows)
    gram = exchange(copies, dp)
    row = scores(tokens, gram, grams)
    row = to_all(row, dp, DP)
    row = jnp.sum(row, axis=0)
    rows = to_all(row, tensor, NY * NC)[:, 0]
    quantized = quantize(bit_widths, x, weight, (over_z, left, right, far0, far1))
    count = row[0, 4 * NB]
    scale = jnp.array([l * l / (OUT * BLK) for l in LEVELS], jnp.float32) / count
    block_errors = rows[:, : 4 * NB].reshape(-1, 4) * scale
    return quantized, own / count, block_errors


def solution(mesh):
    fine = Mesh(mesh.devices.reshape(NX, NZ, NY, NC), ("x", "z", "y", "c"))
    dp = ("x", "z")
    tensor = ("y", "c")
    placed = (P(dp, tensor), P(dp), P(dp, tensor), P(tensor, dp, None), P(tensor))
    return jax.shard_map(
        per_device,
        mesh=fine,
        in_specs=placed,
        out_specs=(P(dp, tensor), P(tensor, dp, None), P()),
        check_vma=False,
    )
```

time: 413 us -> 141 us (0.34); the launches traced: 405 us -> 140 us
  blocking collectives: 175 us -> 18.7 us
  matrix products: 92.2 us -> 0 us
  starting transfers between devices: 0.08 us -> 51.3 us
  waiting for transfers between devices: 68.8 us -> 29.4 us
  Pallas kernels: 0 us -> 32.8 us
  between operations: 30 us -> 0.8 us
  other arithmetic: 18.7 us -> 1.94 us
  local copies, waits for them, and re-layouts: 20.2 us -> 4.8 us
    psum x2 -> x0, blocking collectives: 127 us -> none  [the longest x1 68.5 us: per_device(): gram_sum, count = lax.psum((partial_gram, live_local), 'dp')]
    dot_general x12 -> x0, matrix products: 92.2 us -> none  [the longest x4 75.6 us: per_device(): jnp.einsum('rbi,bij->rbj', delta, gram, precision=lax.Precision.HIGHEST)]
    psum x1 -> x0, waiting for transfers between devices: 68.8 us -> none  [per_device(): gram_sum, count = lax.psum((partial_gram, live_local), 'dp')]
    all_gather x1 -> x0, blocking collectives: 48.2 us -> none  [per_device(): block_errors = lax.all_gather(summed_rows, 'tensor', axis=0, tiled=True)]
    all_to_all x0 -> x4, starting transfers between devices: none -> 38.8 us  [exchange(): return lax.all_to_all(pieces, axes, 0, 0, tiled=False)]
    pallas_call x0 -> x6, Pallas kernels: none -> 32.8 us  [the longest x1 10.5 us: error_grams(): pl.pallas_call(error_kernel, out_shape=jax.ShapeDtypeStruct((NB, 4, DP, R...]
    all_to_all x0 -> x1, blocking collectives: none -> 18.7 us  [exchange(): return lax.all_to_all(pieces, axes, 0, 0, tiled=False)]
    all_to_all x0 -> x4, waiting for transfers between devices: none -> 17 us  [exchange(): return lax.all_to_all(pieces, axes, 0, 0, tiled=False)]
  transfers between devices with their start and end apart: 2 -> 8, of which waited for: 1 -> 4; matrix products, arithmetic and copies ran while one was open for 22% -> 2% of each run, Pallas kernels for 0% -> 21%
where the time goes in v1:
time: 141 us; the launch traced here: 140 us
  starting transfers between devices  51.3 us (36%)
  Pallas kernels  32.8 us (23%)
  waiting for transfers between devices  29.4 us (21%)
  blocking collectives  18.7 us (13%)
  local copies, waits for them, and re-layouts  4.8 us (3%)
  other arithmetic  1.94 us (1%)
    all_to_all x4, starting transfers between devices, exchange(): return lax.all_to_all(pieces, axes, 0, 0, tiled=False)  38.8 us
    all_to_all x1, blocking collectives, exchange(): return lax.all_to_all(pieces, axes, 0, 0, tiled=False)  18.7 us
    all_to_all x4, waiting for transfers between devices, exchange(): return lax.all_to_all(pieces, axes, 0, 0, tiled=False)  17 us
    ppermute x4, starting transfers between devices, shift_x(): return lax.ppermute(piece, 'x', [(i, (i + by) % NX) for i in range(NX)])  12.5 us
    ppermute x4, waiting for transfers between devices, shift_x(): return lax.ppermute(piece, 'x', [(i, (i + by) % NX) for i in range(NX)])  12.4 us
    pallas_call x1, Pallas kernels, error_grams(): pl.pallas_call(error_kernel, out_shape=jax.ShapeDtypeStruct((NB, 4, DP, R...  10.5 us
    pallas_call x1, Pallas kernels, quantize(): pl.pallas_call(quant_kernel, out_shape=jax.ShapeDtypeStruct((rows, PANEL)...  6.97 us
    pallas_call x1, Pallas kernels, gram_partial(): pl.pallas_call(gram_kernel, out_shape=jax.ShapeDtypeStruct((DP, NB, ROWS,...  5.92 us
  transfers between devices with their start and end apart: 8, of which 4 were waited for; matrix products, arithmetic and copies ran while one was open for 2% of the time, Pallas kernels for 21%

profile of v1, /device:TPU:1, one launch (start us, length us, event | category | flops | bytes accessed | tf_op | source)
XLA Modules:
  0.0 139.8 jit_solution(17048503605107684833)
XLA Ops:
  0.6 1.8 %pack_factor.1 = f32[8,29,4,128]{3,2,1,0:T(4,128)} custom-call(s32[1]{0:T(128)} %bitcast.1.first_ref, f32[8,4,1024]{2,1,0:T(4,128)} %f_ref.1), custom_call_target="tpu_custom_call" | custom-call | tf_op jit(solution)/shard_map/pack_factor/pallas_call | solution.py:59
  2.4 10.9 %all-to-all-start = ((f32[8,29,4,128]{3,2,1,0:T(4,128)}), f32[8,29,4,128]{3,2,1,0:T(4,128)S(1)}, u32[]{:S(2)}, u32[]{:S(2)}) async-start(f32[8,29,4,128]{3,2,1,0:T(4,128)} %pack_factor.1), calls=%async_computation | async-start | bytes 950272 | tf_op jit(solution)/shard_map/all_to_all | solution.py:257
  13.3 5.9 %gram_partial.1 = f32[32,8,4,128]{3,2,1,0:T(4,128)} custom-call(s32[1,512]{1,0:T(1,128)} %bitcast.15, bf16[512,1024]{1,0:T(8,128)(2,1)} %a_ref.1), custom_call_target="tpu_custom_call" | custom-call | tf_op jit(solution)/shard_map/gram_partial/pallas_call | solution.py:82
  19.2 10.9 %all-to-all-done.own_ref = f32[8,29,4,128]{3,2,1,0:T(4,128)S(1)} async-done(((f32[8,29,4,128]{3,2,1,0:T(4,128)}), f32[8,29,4,128]{3,2,1,0:T(4,128)S(1)}, u32[]{:S(2)}, u32[]{:S(2)}) %all-to-all-start) | async-done | bytes 475168 | tf_op jit(solution)/shard_map/all_to_all | solution.py:257
  30.1 18.7 %all_to_all.25.g_ref = f32[32,8,4,128]{3,2,1,0:T(4,128)} all-to-all(f32[32,8,4,128]{3,2,1,0:T(4,128)} %gram_partial.1), channel_id=1, replica_groups=mesh['x'=4,'z'=8,'y'=8,'c'=2] {'x','z'}, dimensions={0} | all-to-all | bytes 1048576 | tf_op jit(solution)/shard_map/all_to_all | solution.py:257
  48.9 2.0 %sum_rows.1 = (f32[8,4,128]{2,1,0:T(4,128)}, f32[32,8,4,128]{3,2,1,0:T(4,128)}) custom-call(f32[32,8,4,128]{3,2,1,0:T(4,128)} %all_to_all.25.g_ref), custom_call_target="tpu_custom_call" | custom-call | tf_op jit(solution)/shard_map/sum_rows/pallas_call | solution.py:106
  50.8 8.1 %all-to-all-start.2 = ((f32[32,8,4,128]{3,2,1,0:T(4,128)}), f32[32,8,4,128]{3,2,1,0:T(4,128)S(1)}, u32[]{:S(2)}, u32[]{:S(2)}) async-start(f32[32,8,4,128]{3,2,1,0:T(4,128)} %get-tuple-element.10), calls=%async_computation.2 | async-start | bytes 1048576 | tf_op jit(solution)/shard_map/all_to_all | solution.py:257
  58.9 4.4 %collective-permute-start.1 = (f32[8,29,4,128]{3,2,1,0:T(4,128)S(1)}, f32[8,29,4,128]{3,2,1,0:T(4,128)S(1)}, u32[]{:S(2)}, u32[]{:S(2)}) collective-permute-start(f32[8,29,4,128]{3,2,1,0:T(4,128)S(1)} %all-to-all-done.own_ref), channel_id=1, source_target_pairs={{0,384},{128,0},{256,128},{384,256},{1,385},{129,1},{257,129},{385... | collective-permute-start | bytes 1425416 | tf_op jit(solution)/shard_map/ppermute | solution.py:265
  63.3 1.9 %collective-permute-start = (f32[8,29,4,128]{3,2,1,0:T(4,128)S(1)}, f32[8,29,4,128]{3,2,1,0:T(4,128)S(1)}, u32[]{:S(2)}, u32[]{:S(2)}) collective-permute-start(f32[8,29,4,128]{3,2,1,0:T(4,128)S(1)} %all-to-all-done.own_ref), channel_id=1, source_target_pairs={{0,128},{128,256},{256,384},{384,0},{1,129},{129,257},{257,385},{3... | collective-permute-start | bytes 1425416 | tf_op jit(solution)/shard_map/ppermute | solution.py:265
  65.2 12.4 %collective-permute-done.1.right_ref = f32[8,29,4,128]{3,2,1,0:T(4,128)S(1)} collective-permute-done((f32[8,29,4,128]{3,2,1,0:T(4,128)S(1)}, f32[8,29,4,128]{3,2,1,0:T(4,128)S(1)}, u32[]{:S(2)}, u32[]{:S(2)}) %collective-permute-start.1) | collective-permute-done | bytes 475168 | tf_op jit(solution)/shard_map/ppermute | solution.py:265
  77.7 4.3 %collective-permute-start.3 = (f32[4,29,4,128]{3,2,1,0:T(4,128)S(1)}, f32[4,29,4,128]{3,2,1,0:T(4,128)S(1)}, u32[]{:S(2)}, u32[]{:S(2)}) collective-permute-start(f32[4,29,4,128]{3,2,1,0:T(4,128)S(1)} %slice.17), channel_id=1, source_target_pairs={{0,384},{128,0},{256,128},{384,256},{1,385},{129,1},{257,129},{385... | collective-permute-start | bytes 712712 | tf_op jit(solution)/shard_map/ppermute | solution.py:265
  82.0 0.0 collective-permute-done.left_ref
  82.0 1.9 %collective-permute-start.2 = (f32[4,29,4,128]{3,2,1,0:T(4,128)S(1)}, f32[4,29,4,128]{3,2,1,0:T(4,128)S(1)}, u32[]{:S(2)}, u32[]{:S(2)}) collective-permute-start(f32[4,29,4,128]{3,2,1,0:T(4,128)S(1)} %slice.16), channel_id=1, source_target_pairs={{0,128},{128,256},{256,384},{384,0},{1,129},{129,257},{257,385},{3... | collective-permute-start | bytes 712712 | tf_op jit(solution)/shard_map/ppermute | solution.py:265
  83.9 10.5 %error_grams.1.s_ref = f32[8,4,32,4,128]{4,3,2,1,0:T(4,128)} custom-call(bf16[512,1024]{1,0:T(8,128)(2,1)} %w_ref.3), custom_call_target="tpu_custom_call" | custom-call | tf_op jit(solution)/shard_map/error_grams/pallas_call | solution.py:134
  94.4 0.0 all-to-all-done.2.g_ref
  94.4 0.8 copy-done
  95.2 5.7 %scores.1 = f32[1,128]{1,0:T(1,128)} custom-call(s32[1,512]{1,0:T(1,128)} %bitcast.16, f32[32,8,4,128]{3,2,1,0:T(4,128)} %copy-done, f32[8,4,32,4,128]{4,3,2,1,0:T(4,128)} %error_grams.1.s_ref), custom_call_target="tpu_custom_call" | custom-call | tf_op jit(solution)/shard_map/scores/pallas_call | solution.py:165
  100.9 0.0 copy-start.7
  100.9 1.3 broadcast_in_dim.7
  102.2 9.6 %all-to-all-start.3 = ((f32[32,1,128]{2,1,0:T(1,128)}), f32[32,1,128]{2,1,0:T(1,128)S(1)}, u32[]{:S(2)}, u32[]{:S(2)}) async-start(f32[32,1,128]{2,1,0:T(1,128)} %broadcast_in_dim.7), calls=%async_computation.3 | async-start | bytes 32768 | tf_op jit(solution)/shard_map/all_to_all | solution.py:257
  111.8 0.7 copy-done.4
  112.5 0.1 copy-done.5
  112.5 7.0 %quantize.1 = bf16[512,1024]{1,0:T(8,128)(2,1)} custom-call(s32[8]{0:T(128)} %bits_ref.1, s32[1]{0:T(128)} %bitcast.x_ref, bf16[512,1024]{1,0:T(8,128)(2,1)} %w_ref.3, f32[8,29,4,128]{3,2,1,0:T(4,128)} %copy-done.1, f32[8,29,4,128]{3,2,1,0:T(4,128)} %copy-done.3, f32[8,29,4,128]{3,2,1,0:T(4,128)} %copy-done.2, f32[4,29,4,128]{3,2,1,0:T(4,128)} %copy-done.5, ...), custom_call_target="tpu_custom_call" | custom-call | tf_op jit(solution)/shard_map/quantize/pallas_call | solution.py:237
  119.5 0.9 all-to-all-done.3
  120.4 0.6 slice.14
  121.0 0.6 broadcast_in_dim.8
  121.6 10.3 %all-to-all-start.4 = ((f32[16,1,128]{2,1,0:T(1,128)}), f32[16,1,128]{2,1,0:T(1,128)S(1)}, u32[]{:S(2)}, u32[]{:S(2)}) async-start(f32[16,1,128]{2,1,0:T(1,128)} %broadcast_in_dim.8), calls=%async_computation.4 | async-start | bytes 16384 | tf_op jit(solution)/shard_map/all_to_all | solution.py:257
  132.0 1.3 broadcast_divide_fusion
  133.2 0.6 broadcast_divide_fusion.1
  133.9 5.1 %all-to-all-done.4 = f32[16,1,128]{2,1,0:T(1,128)S(1)} async-done(((f32[16,1,128]{2,1,0:T(1,128)}), f32[16,1,128]{2,1,0:T(1,128)S(1)}, u32[]{:S(2)}, u32[]{:S(2)}) %all-to-all-start.4) | async-done | bytes 8224 | tf_op jit(solution)/shard_map/all_to_all | solution.py:257
  139.0 0.1 reshape.30
  139.1 0.7 copy.13
  (18 shorter events, 0.1 us)
Async XLA Ops:
  2.4 27.7 %all-to-all-start = ((f32[8,29,4,128]{3,2,1,0:T(4,128)}), f32[8,29,4,128]{3,2,1,0:T(4,128)S(1)}, u32[]{:S(2)}, u32[]{:S(2)}) async-start(f32[8,29,4,128]{3,2,1,0:T(4,128)} %pack_factor.1), calls=%async_computation | async-start | bytes 950272 | tf_op jit(solution)/shard_map/all_to_all | solution.py:257
  30.1 64.3 %copy-start.1 = (f32[8,29,4,128]{3,2,1,0:T(4,128)}, f32[8,29,4,128]{3,2,1,0:T(4,128)S(1)}, u32[]{:S(2)}) copy-start(f32[8,29,4,128]{3,2,1,0:T(4,128)S(1)} %all-to-all-done.own_ref) | copy-start | bytes 1425412
  50.8 43.6 %all-to-all-start.2 = ((f32[32,8,4,128]{3,2,1,0:T(4,128)}), f32[32,8,4,128]{3,2,1,0:T(4,128)S(1)}, u32[]{:S(2)}, u32[]{:S(2)}) async-start(f32[32,8,4,128]{3,2,1,0:T(4,128)} %get-tuple-element.10), calls=%async_computation.2 | async-start | bytes 1048576 | tf_op jit(solution)/shard_map/all_to_all | solution.py:257
  58.9 18.7 %collective-permute-start.1 = (f32[8,29,4,128]{3,2,1,0:T(4,128)S(1)}, f32[8,29,4,128]{3,2,1,0:T(4,128)S(1)}, u32[]{:S(2)}, u32[]{:S(2)}) collective-permute-start(f32[8,29,4,128]{3,2,1,0:T(4,128)S(1)} %all-to-all-done.own_ref), channel_id=1, source_target_pairs={{0,384},{128,0},{256,128},{384,256},{1,385},{129,1},{257,129},{385... | collective-permute-start | bytes 1425416 | tf_op jit(solution)/shard_map/ppermute | solution.py:265
  63.3 18.6 %collective-permute-start = (f32[8,29,4,128]{3,2,1,0:T(4,128)S(1)}, f32[8,29,4,128]{3,2,1,0:T(4,128)S(1)}, u32[]{:S(2)}, u32[]{:S(2)}) collective-permute-start(f32[8,29,4,128]{3,2,1,0:T(4,128)S(1)} %all-to-all-done.own_ref), channel_id=1, source_target_pairs={{0,128},{128,256},{256,384},{384,0},{1,129},{129,257},{257,385},{3... | collective-permute-start | bytes 1425416 | tf_op jit(solution)/shard_map/ppermute | solution.py:265
  77.6 23.2 %copy-start.2 = (f32[8,29,4,128]{3,2,1,0:T(4,128)}, f32[8,29,4,128]{3,2,1,0:T(4,128)S(1)}, u32[]{:S(2)}) copy-start(f32[8,29,4,128]{3,2,1,0:T(4,128)S(1)} %collective-permute-done.1.right_ref) | copy-start | bytes 1425412
  77.7 34.1 %collective-permute-start.3 = (f32[4,29,4,128]{3,2,1,0:T(4,128)S(1)}, f32[4,29,4,128]{3,2,1,0:T(4,128)S(1)}, u32[]{:S(2)}, u32[]{:S(2)}) collective-permute-start(f32[4,29,4,128]{3,2,1,0:T(4,128)S(1)} %slice.17), channel_id=1, source_target_pairs={{0,384},{128,0},{256,128},{384,256},{1,385},{129,1},{257,129},{385... | collective-permute-start | bytes 712712 | tf_op jit(solution)/shard_map/ppermute | solution.py:265
  82.0 18.9 %copy-start.3 = (f32[8,29,4,128]{3,2,1,0:T(4,128)}, f32[8,29,4,128]{3,2,1,0:T(4,128)S(1)}, u32[]{:S(2)}) copy-start(f32[8,29,4,128]{3,2,1,0:T(4,128)S(1)} %collective-permute-done.left_ref) | copy-start | bytes 1425412
  82.0 29.8 %collective-permute-start.2 = (f32[4,29,4,128]{3,2,1,0:T(4,128)S(1)}, f32[4,29,4,128]{3,2,1,0:T(4,128)S(1)}, u32[]{:S(2)}, u32[]{:S(2)}) collective-permute-start(f32[4,29,4,128]{3,2,1,0:T(4,128)S(1)} %slice.16), channel_id=1, source_target_pairs={{0,128},{128,256},{256,384},{384,0},{1,129},{129,257},{257,385},{3... | collective-permute-start | bytes 712712 | tf_op jit(solution)/shard_map/ppermute | solution.py:265
  94.4 0.8 copy-start
  100.9 31.1 %copy-start.6 = (f32[8,4,128]{2,1,0:T(4,128)S(1)}, f32[8,4,128]{2,1,0:T(4,128)}, u32[]{:S(2)}) copy-start(f32[8,4,128]{2,1,0:T(4,128)} %get-tuple-element.9) | copy-start | bytes 49156
  100.9 32.3 %copy-start.7 = (f32[4]{0:T(128)S(1)}, f32[4]{0:T(128)}, u32[]{:S(2)}) copy-start(f32[4]{0:T(128)} %constant.19.clone) | copy-start | bytes 52
  102.2 18.2 %all-to-all-start.3 = ((f32[32,1,128]{2,1,0:T(1,128)}), f32[32,1,128]{2,1,0:T(1,128)S(1)}, u32[]{:S(2)}, u32[]{:S(2)}) async-start(f32[32,1,128]{2,1,0:T(1,128)} %broadcast_in_dim.7), calls=%async_computation.3 | async-start | bytes 32768 | tf_op jit(solution)/shard_map/all_to_all | solution.py:257
  111.8 0.7 copy-start.4
  111.8 0.8 copy-start.5
  121.6 17.4 %all-to-all-start.4 = ((f32[16,1,128]{2,1,0:T(1,128)}), f32[16,1,128]{2,1,0:T(1,128)S(1)}, u32[]{:S(2)}, u32[]{:S(2)}) async-start(f32[16,1,128]{2,1,0:T(1,128)} %broadcast_in_dim.8), calls=%async_computation.4 | async-start | bytes 16384 | tf_op jit(solution)/shard_map/all_to_all | solution.py:257

commit v2 on v1

--- a/solution.py
+++ b/solution.py
@@ -40,7 +40,7 @@
     return pltpu.CompilerParams(dimension_semantics=semantics, vmem_limit_bytes=56 << 20)
 
 
-def pack_kernel(first_ref, f_ref, o_ref):
+def pack_kernel(first_ref, f_ref, tok_ref, a_ref, o_ref):
     lane = lax.broadcasted_iota(jnp.int32, (ROWS, BLK), 1)
     row = lax.broadcasted_iota(jnp.int32, (ROWS, BLK), 0)
     on_diag = lane == row + first_ref[0]
@@ -50,69 +50,73 @@
         value = jnp.sum(jnp.where(on_diag, tile, 0.0), axis=1, keepdims=True)
         diag = jnp.where(lane == j, value, diag)
     for i in range(NZ):
-        for p, (j, c) in enumerate(PAIRS):
-            o_ref[i, p] = f_ref[j, :, c * BLK : (c + 1) * BLK]
         o_ref[i, NP - 1] = diag
-
-
-def pack_factor(first, factor):
+    for p, (j, c) in enumerate(PAIRS):
+        tile = f_ref[j, :, c * BLK : (c + 1) * BLK]
+        for i in range(NZ):
+            o_ref[i, p] = tile
+    live = jnp.where(tok_ref[...] != PAD, 1.0, 0.0).astype(jnp.bfloat16)
+    for b in range(NB):
+        x = a_ref[:, b * BLK : (b + 1) * BLK]
+        g = jnp.dot(x.T * live, x, preferred_element_type=jnp.float32)
+        for d in range(DP):
+            o_ref[d % NZ, NP + (d // NZ) * NB + b] = g[d * ROWS : (d + 1) * ROWS]
+
+
+def pack(first, factor, tokens, activations):
+    vmem = pl.BlockSpec(memory_space=pltpu.VMEM)
     return pl.pallas_call(
         pack_kernel,
-        out_shape=jax.ShapeDtypeStruct((NZ, NP, ROWS, BLK), jnp.float32),
-        in_specs=[
-            pl.BlockSpec(memory_space=pltpu.SMEM),
-            pl.BlockSpec(memory_space=pltpu.VMEM),
-        ],
-        out_specs=pl.BlockSpec(memory_space=pltpu.VMEM),
-        compiler_params=params(),
-        name="pack_factor",
-    )(first, factor)
-
-
-def gram_kernel(tok_ref, a_ref, o_ref):
-    live = jnp.where(tok_ref[...] != PAD, 1.0, 0.0).astype(jnp.bfloat16)
-    x = a_ref[...]
-    g = jnp.dot(x.T * live, x, preferred_element_type=jnp.float32)
-    for d in range(DP):
-        o_ref[d, 0] = g[d * ROWS : (d + 1) * ROWS]
-
-
-def gram_partial(tokens, activations):
-    n = activations.shape[0]
-    return pl.pallas_call(
-        gram_kernel,
-        out_shape=jax.ShapeDtypeStruct((DP, NB, ROWS, BLK), jnp.float32),
-        grid=(NB,),
-        in_specs=[
-            pl.BlockSpec((1, n), lambda b: (0, 0)),
-            pl.BlockSpec((n, BLK), lambda b: (0, b)),
-        ],
-        out_specs=pl.BlockSpec((DP, 1, ROWS, BLK), lambda b: (0, b, 0, 0)),
-        compiler_params=params("arbitrary"),
-        name="gram_partial",
-    )(tokens, activations)
-
-
-def sum_kernel(g_ref, own_ref, o_ref):
+        out_shape=jax.ShapeDtypeStruct((NZ, NP + NX * NB, ROWS, BLK), jnp.float32),
+        in_specs=[pl.BlockSpec(memory_space=pltpu.SMEM), vmem, vmem, vmem],
+        out_specs=vmem,
+        compiler_params=params(),
+        name="pack",
+    )(first, factor, tokens, activations)
+
+
+def sum_z_kernel(g_ref, o_ref):
+    for x in range(NX):
+        tiles = slice(NP + x * NB, NP + (x + 1) * NB)
+        total = g_ref[0, tiles]
+        for i in range(1, NZ):
+            total = total + g_ref[i, tiles]
+        o_ref[x] = total
+
+
+def sum_z(received):
+    vmem = pl.BlockSpec(memory_space=pltpu.VMEM)
+    return pl.pallas_call(
+        sum_z_kernel,
+        out_shape=jax.ShapeDtypeStruct((NX, NB, ROWS, BLK), jnp.float32),
+        in_specs=[vmem],
+        out_specs=vmem,
+        compiler_params=params(),
+        name="sum_z",
+    )(received)
+
+
+def sum_x_kernel(g_ref, own_ref, o_ref):
     total = g_ref[0]
-    for d in range(1, DP):
-        total = total + g_ref[d]
+    for x in range(1, NX):
+        total = total + g_ref[x]
     own_ref[...] = total
     for d in range(DP):
         o_ref[d] = total
 
 
-def sum_rows(received):
-    return pl.pallas_call(
-        sum_kernel,
+def sum_x(received):
+    vmem = pl.BlockSpec(memory_space=pltpu.VMEM)
+    return pl.pallas_call(
+        sum_x_kernel,
         out_shape=(
             jax.ShapeDtypeStruct((NB, ROWS, BLK), jnp.float32),
             jax.ShapeDtypeStruct((DP, NB, ROWS, BLK), jnp.float32),
         ),
-        in_specs=[pl.BlockSpec(memory_space=pltpu.VMEM)],
-        out_specs=(pl.BlockSpec(memory_space=pltpu.VMEM),) * 2,
-        compiler_params=params(),
-        name="sum_rows",
+        in_specs=[vmem],
+        out_specs=(vmem, vmem),
+        compiler_params=params(),
+        name="sum_x",
     )(received)
 
 
@@ -142,52 +146,105 @@
     )(weight)
 
 
-def score_kernel(tok_ref, g_ref, s_ref, o_ref):
-    b = pl.program_id(0)
-    lane = lax.broadcasted_iota(jnp.int32, (1, BLK), 1)
-
-    @pl.when(b == 0)
-    def _():
-        live = jnp.sum(jnp.where(tok_ref[...] != PAD, 1.0, 0.0))
-        o_ref[...] = jnp.where(lane == 4 * NB, live, 0.0)
-
-    row = o_ref[...]
-    for k in range(4):
-        acc = g_ref[0, 0] * s_ref[0, k, 0]
-        for d in range(1, DP):
-            acc = acc + g_ref[d, 0] * s_ref[0, k, d]
-        row = jnp.where(lane == 4 * b + k, jnp.sum(acc), row)
-    o_ref[...] = row
+def score_kernel(tok_ref, g_ref, s_ref, o_ref, row_ref):
+    row_ref[...] = jnp.zeros((BLK, BLK), jnp.float32)
+    live = jnp.where(tok_ref[...] != PAD, 1.0, 0.0)
+    row_ref[4 * NB : 4 * NB + 1, :] = sum(live[:, i : i + BLK] for i in range(0, live.shape[1], BLK))
+    for b in range(NB):
+        for k in range(4):
+            acc = g_ref[0, b] * s_ref[b, k, 0]
+            for d in range(1, DP):
+                acc = acc + g_ref[d, b] * s_ref[b, k, d]
+            row_ref[k * NB + b : k * NB + b + 1, :] = jnp.sum(acc, axis=0, keepdims=True)
+    row = jnp.sum(row_ref[...].T, axis=0, keepdims=True)
+    for d in range(DP):
+        o_ref[d] = row
 
 
 def scores(tokens, gram, grams):
-    n = tokens.shape[1]
+    vmem = pl.BlockSpec(memory_space=pltpu.VMEM)
     return pl.pallas_call(
         score_kernel,
-        out_shape=jax.ShapeDtypeStruct((1, BLK), jnp.float32),
-        grid=(NB,),
-        in_specs=[
-            pl.BlockSpec((1, n), lambda b: (0, 0)),
-            pl.BlockSpec((DP, 1, ROWS, BLK), lambda b: (0, b, 0, 0)),
-            pl.BlockSpec((1, 4, DP, ROWS, BLK), lambda b: (b, 0, 0, 0, 0)),
-        ],
-        out_specs=pl.BlockSpec((1, BLK), lambda b: (0, 0)),
-        compiler_params=params("arbitrary"),
+        out_shape=jax.ShapeDtypeStruct((DP, 1, BLK), jnp.float32),
+        in_specs=[vmem] * 3,
+        out_specs=vmem,
+        scratch_shapes=[pltpu.VMEM((BLK, BLK), jnp.float32)],
+        compiler_params=params(),
         name="scores",
     )(tokens, gram, grams)
 
 
+def total_kernel(r_ref, own_ref, gram_ref, o_ref):
+    row = r_ref[0]
+    for d in range(1, DP):
+        row = row + r_ref[d]
+    lane = lax.broadcasted_iota(jnp.int32, (1, BLK), 1)
+    count = jnp.sum(jnp.where(lane == 4 * NB, row, 0.0))
+    gram_ref[...] = own_ref[...] / count
+    scale = jnp.zeros((1, BLK), jnp.float32)
+    for k, levels in enumerate(LEVELS):
+        scale = jnp.where(lane // NB == k, levels * levels / (OUT * BLK), scale)
+    row = row * scale / count
+    for t in range(NY * NC):
+        o_ref[t] = row
+
+
+def totals(rows, own):
+    vmem = pl.BlockSpec(memory_space=pltpu.VMEM)
+    return pl.pallas_call(
+        total_kernel,
+        out_shape=(
+            jax.ShapeDtypeStruct((NB, ROWS, BLK), jnp.float32),
+            jax.ShapeDtypeStruct((NY * NC, 1, BLK), jnp.float32),
+        ),
+        in_specs=[vmem, vmem],
+        out_specs=(vmem, vmem),
+        compiler_params=params(),
+        name="totals",
+    )(rows, own)
+
+
+def spread_kernel(r_ref, o_ref, row_ref):
+    n = NY * NC
+    for t in range(n):
+        row_ref[t : t + 1, :] = r_ref[t]
+    lane = lax.broadcasted_iota(jnp.int32, (8, BLK), 1)
+    source = lax.broadcasted_iota(jnp.int32, (8, BLK), 0)
+    total = [jnp.zeros((1, BLK), jnp.float32)] * 4
+    for h in range(n // 8):
+        skewed = pltpu.roll(row_ref[h * 8 : (h + 1) * 8, :], 0, 1, stride=NB, stride_axis=0)
+        for k in range(4):
+            moved = pltpu.roll(skewed, (h * 8 * NB - k * NB) % BLK, 1)
+            kept = jnp.where(lane // NB == source + h * 8, moved, 0.0)
+            total[k] = total[k] + jnp.sum(kept, axis=0, keepdims=True)
+    for k in range(4):
+        o_ref[k : k + 1, :] = total[k]
+
+
+def spread(rows):
+    vmem = pl.BlockSpec(memory_space=pltpu.VMEM)
+    return pl.pallas_call(
+        spread_kernel,
+        out_shape=jax.ShapeDtypeStruct((4, BLK), jnp.float32),
+        in_specs=[vmem],
+        out_specs=vmem,
+        scratch_shapes=[pltpu.VMEM((NY * NC, BLK), jnp.float32)],
+        compiler_params=params(),
+        name="spread",
+    )(rows)
+
+
 CHUNKS = 2
 
 
-def quant_kernel(bits_ref, x_ref, w_ref, own_ref, left_ref, right_ref, far0_ref, far1_ref, o_ref, c_ref, u_ref, slab_ref):
+def quant_kernel(bits_ref, x_ref, w_ref, own_ref, left_ref, right_ref, far_ref, o_ref, c_ref, u_ref, slab_ref):
     rows = w_ref.shape[0] // CHUNKS
     x = x_ref[0]
 
     def slab(p):
-        for off, refs in ((0, (own_ref,)), (NX - 1, (left_ref,)), (1, (right_ref,)), (2, (far0_ref, far1_ref))):
+        for off, ref in enumerate((own_ref, right_ref, far_ref, left_ref)):
             base = pl.multiple_of(lax.rem(x + off, NX) * (NZ * ROWS), NZ * ROWS)
-            chunk = jnp.concatenate([ref[i, p] for ref in refs for i in range(ref.shape[0])], axis=0)
+            chunk = jnp.concatenate([ref[i, p] for i in range(NZ)], axis=0)
             slab_ref[pl.ds(base, NZ * ROWS), :] = chunk
         return slab_ref[...]
 
@@ -241,7 +298,7 @@
             pl.BlockSpec(memory_space=pltpu.SMEM),
             pl.BlockSpec(memory_space=pltpu.SMEM),
         ]
-        + [pl.BlockSpec(memory_space=pltpu.VMEM)] * 6,
+        + [pl.BlockSpec(memory_space=pltpu.VMEM)] * 5,
         out_specs=pl.BlockSpec(memory_space=pltpu.VMEM),
         scratch_shapes=[
             pltpu.VMEM((rows, PANEL), jnp.float32),
@@ -257,10 +314,6 @@
     return lax.all_to_all(pieces, axes, 0, 0, tiled=False)
 
 
-def to_all(piece, axes, count):
-    return exchange(jnp.broadcast_to(piece[None], (count,) + piece.shape), axes)
-
-
 def shift_x(piece, by):
     return lax.ppermute(piece, "x", [(i, (i + by) % NX) for i in range(NX)])
 
@@ -268,31 +321,29 @@
 def per_device(activations, token_ids, weight, inv_chol, bit_widths):
     dp = ("x", "z")
     tensor = ("y", "c")
-    half = NZ // 2
     tokens = token_ids.reshape(1, -1)
     x = lax.axis_index("x").reshape(1).astype(jnp.int32)
     first = (lax.axis_index(dp) * ROWS).reshape(1).astype(jnp.int32)
-    packed = pack_factor(first, inv_chol)
+    packed = pack(first, inv_chol, tokens, activations)
     over_z = exchange(packed, "z")
-    partial = gram_partial(tokens, activations)
     grams = error_grams(weight)
-    over_z, partial = lax.optimization_barrier((over_z, partial))
-    gram_rows = exchange(partial, dp)
-    left = shift_x(over_z, 1)
-    right = shift_x(over_z, -1)
-    far0 = shift_x(left[:half], 1)
-    far1 = shift_x(right[half:], -1)
-    own, copies = sum_rows(gram_rows)
+    rows = sum_z(over_z)
+    rows = exchange(rows, "x")
+    own, copies = sum_x(rows)
     gram = exchange(copies, dp)
+    mine, _ = lax.optimization_barrier((over_z, copies))
+    mine = mine[:, :NP]
+    left = shift_x(mine, 1)
+    right = shift_x(mine, -1)
     row = scores(tokens, gram, grams)
-    row = to_all(row, dp, DP)
-    row = jnp.sum(row, axis=0)
-    rows = to_all(row, tensor, NY * NC)[:, 0]
-    quantized = quantize(bit_widths, x, weight, (over_z, left, right, far0, far1))
-    count = row[0, 4 * NB]
-    scale = jnp.array([l * l / (OUT * BLK) for l in LEVELS], jnp.float32) / count
-    block_errors = rows[:, : 4 * NB].reshape(-1, 4) * scale
-    return quantized, own / count, block_errors
+    left_late, _ = lax.optimization_barrier((left, row))
+    row = exchange(row, dp)
+    far = shift_x(left_late, 1)
+    gram_out, row = totals(row, own)
+    rows = exchange(row, tensor)
+    quantized = quantize(bit_widths, x, weight, (mine, left, right, far))
+    block_errors = spread(rows).T
+    return quantized, gram_out, block_errors
 
 
 def solution(mesh):

time: 141 us -> 130 us (0.922)
  blocking collectives: 18.7 us -> 83.8 us
  starting transfers between devices: 51.3 us -> 12.3 us
  waiting for transfers between devices: 29.4 us -> 0.01 us
  Pallas kernels: 32.8 us -> 29.6 us
  local copies, waits for them, and re-layouts: 4.8 us -> 2.8 us
  other arithmetic: 1.94 us -> 0 us
    all_to_all x1 -> x4, blocking collectives: 18.7 us -> 83.8 us  [exchange(): return lax.all_to_all(pieces, axes, 0, 0, tiled=False)]
    all_to_all x4 -> x1, starting transfers between devices: 38.8 us -> 3.89 us  [exchange(): return lax.all_to_all(pieces, axes, 0, 0, tiled=False)]
    all_to_all x4 -> x1, waiting for transfers between devices: 17 us -> 0.01 us  [exchange(): return lax.all_to_all(pieces, axes, 0, 0, tiled=False)]
    ppermute x4 -> x3, waiting for transfers between devices: 12.4 us -> 0.01 us  [shift_x(): return lax.ppermute(piece, 'x', [(i, (i + by) % NX) for i in range(NX)])]
    ppermute x4 -> x3, starting transfers between devices: 12.5 us -> 8.4 us  [shift_x(): return lax.ppermute(piece, 'x', [(i, (i + by) % NX) for i in range(NX)])]
    pallas_call x4 -> x6, Pallas kernels: 15.4 us -> 12.2 us  [the longest x1 2.83 us: scores(): pl.pallas_call(score_kernel, out_shape=jax.ShapeDtypeStruct((DP, 1, BLK),...]
    div x2 -> x0, other arithmetic: 1.91 us -> none  [the longest x1 1.26 us: per_device(): return (quantized, own / count, block_errors)]
    broadcast_in_dim x2 -> x0, local copies, waits for them, and re-layouts: 1.89 us -> none  [to_all(): return exchange(jnp.broadcast_to(piece[None], (count,) + piece.shape), axes)]
  transfers between devices with their start and end apart: 8 -> 4, of which waited for: 4 -> 0; matrix products, arithmetic and copies ran while one was open for 2% -> 1% of each run, Pallas kernels for 21% -> 13%
where the time goes in v2:
time: 130 us; the launch traced here: 129 us
  blocking collectives  83.8 us (64%)
  Pallas kernels  29.6 us (23%)
  starting transfers between devices  12.3 us (9%)
  local copies, waits for them, and re-layouts  2.8 us (2%)
    all_to_all x4, blocking collectives, exchange(): return lax.all_to_all(pieces, axes, 0, 0, tiled=False)  83.8 us
    pallas_call x1, Pallas kernels, error_grams(): pl.pallas_call(error_kernel, out_shape=jax.ShapeDtypeStruct((NB, 4, DP, R...  10.5 us
    ppermute x3, starting transfers between devices, shift_x(): return lax.ppermute(piece, 'x', [(i, (i + by) % NX) for i in range(NX)])  8.4 us
    pallas_call x1, Pallas kernels, quantize(): pl.pallas_call(quant_kernel, out_shape=jax.ShapeDtypeStruct((rows, PANEL)...  6.96 us
    all_to_all x1, starting transfers between devices, exchange(): return lax.all_to_all(pieces, axes, 0, 0, tiled=False)  3.89 us
    pallas_call x1, Pallas kernels, scores(): pl.pallas_call(score_kernel, out_shape=jax.ShapeDtypeStruct((DP, 1, BLK),...  2.83 us
    pallas_call x1, Pallas kernels, pack(): pl.pallas_call(pack_kernel, out_shape=jax.ShapeDtypeStruct((NZ, NP + NX *...  2.77 us
  transfers between devices with their start and end apart: 4, of which 0 were waited for; matrix products, arithmetic and copies ran while one was open for 1% of the time, Pallas kernels for 13%

profile of v2, /device:TPU:1, one launch (start us, length us, event | category | flops | bytes accessed | tf_op | source)
XLA Modules:
  0.0 129.3 jit_solution(7094382236695317477)
XLA Ops:
  0.6 2.8 %pack.1 = f32[8,61,4,128]{3,2,1,0:T(4,128)} custom-call(s32[1]{0:T(128)} %bitcast.1.first_ref, f32[8,4,1024]{2,1,0:T(4,128)} %f_ref.1, s32[1,512]{1,0:T(1,128)} %bitcast.4, bf16[512,1024]{1,0:T(8,128)(2,1)} %a_ref.1), custom_call_target="tpu_custom_call" | custom-call | tf_op jit(solution)/shard_map/pack/pallas_call | solution.py:68
  3.4 37.4 %all_to_all.25.g_ref = f32[8,61,4,128]{3,2,1,0:T(4,128)} all-to-all(f32[8,61,4,128]{3,2,1,0:T(4,128)} %pack.1), channel_id=1, replica_groups=mesh['x'=4,'z'=8,'y'=8,'c'=2] {'z'}, dimensions={0} | all-to-all | bytes 1998848 | tf_op jit(solution)/shard_map/all_to_all | solution.py:314
  40.8 1.9 %sum_z.1 = f32[4,8,4,128]{3,2,1,0:T(4,128)} custom-call(f32[8,61,4,128]{3,2,1,0:T(4,128)} %all_to_all.25.g_ref), custom_call_target="tpu_custom_call" | custom-call | tf_op jit(solution)/shard_map/sum_z/pallas_call | solution.py:89
  42.7 8.6 %all_to_all.26.g_ref = f32[4,8,4,128]{3,2,1,0:T(4,128)} all-to-all(f32[4,8,4,128]{3,2,1,0:T(4,128)} %sum_z.1), channel_id=1, replica_groups=mesh['x'=4,'z'=8,'y'=8,'c'=2] {'x'}, dimensions={0} | all-to-all | bytes 131072 | tf_op jit(solution)/shard_map/all_to_all | solution.py:314
  51.2 1.8 %sum_x.1 = (f32[8,4,128]{2,1,0:T(4,128)}, f32[32,8,4,128]{3,2,1,0:T(4,128)}) custom-call(f32[4,8,4,128]{3,2,1,0:T(4,128)} %all_to_all.26.g_ref), custom_call_target="tpu_custom_call" | custom-call | tf_op jit(solution)/shard_map/sum_x/pallas_call | solution.py:110
  53.0 3.9 %all-to-all-start.2 = ((f32[32,8,4,128]{3,2,1,0:T(4,128)}), f32[32,8,4,128]{3,2,1,0:T(4,128)S(1)}, u32[]{:S(2)}, u32[]{:S(2)}) async-start(f32[32,8,4,128]{3,2,1,0:T(4,128)} %get-tuple-element.9), calls=%async_computation.2 | async-start | bytes 1048576 | tf_op jit(solution)/shard_map/all_to_all | solution.py:314
  56.9 1.1 slice.3.own_ref
  58.0 0.0 copy-start.1
  58.0 3.1 %collective-permute-start = (f32[8,29,4,128]{3,2,1,0:T(4,128)S(1)}, f32[8,29,4,128]{3,2,1,0:T(4,128)S(1)}, u32[]{:S(2)}, u32[]{:S(2)}) collective-permute-start(f32[8,29,4,128]{3,2,1,0:T(4,128)S(1)} %slice.3.own_ref), channel_id=1, source_target_pairs={{0,128},{128,256},{256,384},{384,0},{1,129},{129,257},{257,385},{3... | collective-permute-start | bytes 1425416 | tf_op jit(solution)/shard_map/ppermute | solution.py:318
  61.0 10.5 %error_grams.1.s_ref = f32[8,4,32,4,128]{4,3,2,1,0:T(4,128)} custom-call(bf16[512,1024]{1,0:T(8,128)(2,1)} %w_ref.3), custom_call_target="tpu_custom_call" | custom-call | tf_op jit(solution)/shard_map/error_grams/pallas_call | solution.py:138
  71.5 3.4 %collective-permute-start.1 = (f32[8,29,4,128]{3,2,1,0:T(4,128)S(1)}, f32[8,29,4,128]{3,2,1,0:T(4,128)S(1)}, u32[]{:S(2)}, u32[]{:S(2)}) collective-permute-start(f32[8,29,4,128]{3,2,1,0:T(4,128)S(1)} %slice.3.own_ref), channel_id=1, source_target_pairs={{0,384},{128,0},{256,128},{384,256},{1,385},{129,1},{257,129},{385... | collective-permute-start | bytes 1425416 | tf_op jit(solution)/shard_map/ppermute | solution.py:318
  74.9 0.0 all-to-all-done.2.g_ref
  74.9 0.0 copy-start
  74.9 0.8 copy-done
  75.7 2.8 %scores.1 = f32[32,1,128]{2,1,0:T(1,128)} custom-call(s32[1,512]{1,0:T(1,128)} %bitcast.5, f32[32,8,4,128]{3,2,1,0:T(4,128)} %copy-done, f32[8,4,32,4,128]{4,3,2,1,0:T(4,128)} %error_grams.1.s_ref), custom_call_target="tpu_custom_call" | custom-call | tf_op jit(solution)/shard_map/scores/pallas_call | solution.py:166
  78.6 0.0 copy-done.1
  78.6 0.0 collective-permute-done.left_ref
  78.6 0.0 copy-start.2
  78.6 1.9 %collective-permute-start.2 = (f32[8,29,4,128]{3,2,1,0:T(4,128)S(1)}, f32[8,29,4,128]{3,2,1,0:T(4,128)S(1)}, u32[]{:S(2)}, u32[]{:S(2)}) collective-permute-start(f32[8,29,4,128]{3,2,1,0:T(4,128)S(1)} %collective-permute-done.left_ref), channel_id=1, source_target_pairs={{0,128},{128,256},{256,384},{384,0},{1,129},{129,257},{257,385},{3... | collective-permute-start | bytes 1425416 | tf_op jit(solution)/shard_map/ppermute | solution.py:318
  80.5 17.8 %all_to_all.27.r_ref = f32[32,1,128]{2,1,0:T(1,128)} all-to-all(f32[32,1,128]{2,1,0:T(1,128)} %scores.1), channel_id=1, replica_groups=mesh['x'=4,'z'=8,'y'=8,'c'=2] {'x','z'}, dimensions={0} | all-to-all | bytes 32768 | tf_op jit(solution)/shard_map/all_to_all | solution.py:314
  98.3 1.5 %totals.1 = (f32[8,4,128]{2,1,0:T(4,128)}, f32[16,1,128]{2,1,0:T(1,128)}) custom-call(f32[32,1,128]{2,1,0:T(1,128)} %all_to_all.27.r_ref, f32[8,4,128]{2,1,0:T(4,128)} %get-tuple-element.12.own_ref), custom_call_target="tpu_custom_call" | custom-call | tf_op jit(solution)/shard_map/totals/pallas_call | solution.py:194
  99.8 20.1 %all_to_all.28.r_ref = f32[16,1,128]{2,1,0:T(1,128)} all-to-all(f32[16,1,128]{2,1,0:T(1,128)} %get-tuple-element.14), channel_id=1, replica_groups=mesh['x'=4,'z'=8,'y'=8,'c'=2] {'y','c'}, dimensions={0} | all-to-all | bytes 16384 | tf_op jit(solution)/shard_map/all_to_all | solution.py:314
  119.9 1.4 %spread.1 = f32[4,128]{1,0:T(4,128)} custom-call(f32[16,1,128]{2,1,0:T(1,128)} %all_to_all.28.r_ref), custom_call_target="tpu_custom_call" | custom-call | tf_op jit(solution)/shard_map/spread/pallas_call | solution.py:226
  121.3 0.0 collective-permute-done.1.right_ref
  121.3 0.0 copy-start.3
  121.3 0.0 collective-permute-done.2.far_ref
  121.3 0.0 copy-start.4
  121.4 0.0 copy-done.2
  121.4 0.8 copy-done.3
  122.1 0.2 copy-done.4
  122.3 7.0 %quantize.1 = bf16[512,1024]{1,0:T(8,128)(2,1)} custom-call(s32[8]{0:T(128)} %bits_ref.1, s32[1]{0:T(128)} %bitcast.x_ref, bf16[512,1024]{1,0:T(8,128)(2,1)} %w_ref.3, f32[8,29,4,128]{3,2,1,0:T(4,128)} %copy-done.1, f32[8,29,4,128]{3,2,1,0:T(4,128)} %copy-done.2, f32[8,29,4,128]{3,2,1,0:T(4,128)} %copy-done.3, f32[8,29,4,128]{3,2,1,0:T(4,128)} %copy-done.4), custom_call_target="tpu_custom_call" | custom-call | tf_op jit(solution)/shard_map/quantize/pallas_call | solution.py:294
Async XLA Ops:
  53.0 21.9 %all-to-all-start.2 = ((f32[32,8,4,128]{3,2,1,0:T(4,128)}), f32[32,8,4,128]{3,2,1,0:T(4,128)S(1)}, u32[]{:S(2)}, u32[]{:S(2)}) async-start(f32[32,8,4,128]{3,2,1,0:T(4,128)} %get-tuple-element.9), calls=%async_computation.2 | async-start | bytes 1048576 | tf_op jit(solution)/shard_map/all_to_all | solution.py:314
  58.0 20.6 %copy-start.1 = (f32[8,29,4,128]{3,2,1,0:T(4,128)}, f32[8,29,4,128]{3,2,1,0:T(4,128)S(1)}, u32[]{:S(2)}) copy-start(f32[8,29,4,128]{3,2,1,0:T(4,128)S(1)} %slice.3.own_ref) | copy-start | bytes 1425412
  58.0 20.6 %collective-permute-start = (f32[8,29,4,128]{3,2,1,0:T(4,128)S(1)}, f32[8,29,4,128]{3,2,1,0:T(4,128)S(1)}, u32[]{:S(2)}, u32[]{:S(2)}) collective-permute-start(f32[8,29,4,128]{3,2,1,0:T(4,128)S(1)} %slice.3.own_ref), channel_id=1, source_target_pairs={{0,128},{128,256},{256,384},{384,0},{1,129},{129,257},{257,385},{3... | collective-permute-start | bytes 1425416 | tf_op jit(solution)/shard_map/ppermute | solution.py:318
  71.5 49.8 %collective-permute-start.1 = (f32[8,29,4,128]{3,2,1,0:T(4,128)S(1)}, f32[8,29,4,128]{3,2,1,0:T(4,128)S(1)}, u32[]{:S(2)}, u32[]{:S(2)}) collective-permute-start(f32[8,29,4,128]{3,2,1,0:T(4,128)S(1)} %slice.3.own_ref), channel_id=1, source_target_pairs={{0,384},{128,0},{256,128},{384,256},{1,385},{129,1},{257,129},{385... | collective-permute-start | bytes 1425416 | tf_op jit(solution)/shard_map/ppermute | solution.py:318
  74.9 0.8 copy-start
  78.6 42.8 %copy-start.2 = (f32[8,29,4,128]{3,2,1,0:T(4,128)}, f32[8,29,4,128]{3,2,1,0:T(4,128)S(1)}, u32[]{:S(2)}) copy-start(f32[8,29,4,128]{3,2,1,0:T(4,128)S(1)} %collective-permute-done.left_ref) | copy-start | bytes 1425412
  78.6 42.8 %collective-permute-start.2 = (f32[8,29,4,128]{3,2,1,0:T(4,128)S(1)}, f32[8,29,4,128]{3,2,1,0:T(4,128)S(1)}, u32[]{:S(2)}, u32[]{:S(2)}) collective-permute-start(f32[8,29,4,128]{3,2,1,0:T(4,128)S(1)} %collective-permute-done.left_ref), channel_id=1, source_target_pairs={{0,128},{128,256},{256,384},{384,0},{1,129},{129,257},{257,385},{3... | collective-permute-start | bytes 1425416 | tf_op jit(solution)/shard_map/ppermute | solution.py:318
  121.3 0.8 copy-start.3
  121.3 1.0 copy-start.4

commit v3 on v2

--- a/solution.py
+++ b/solution.py
@@ -40,7 +40,28 @@
     return pltpu.CompilerParams(dimension_semantics=semantics, vmem_limit_bytes=56 << 20)
 
 
-def pack_kernel(first_ref, f_ref, tok_ref, a_ref, o_ref):
+def gram_kernel(tok_ref, a_ref, o_ref):
+    live = jnp.where(tok_ref[...] != PAD, 1.0, 0.0).astype(jnp.bfloat16)
+    for b in range(NB):
+        x = a_ref[:, b * BLK : (b + 1) * BLK]
+        g = jnp.dot(x.T * live, x, preferred_element_type=jnp.float32)
+        for d in range(DP):
+            o_ref[d // NZ, d % NZ, b] = g[d * ROWS : (d + 1) * ROWS]
+
+
+def gram_partial(tokens, activations):
+    vmem = pl.BlockSpec(memory_space=pltpu.VMEM)
+    return pl.pallas_call(
+        gram_kernel,
+        out_shape=jax.ShapeDtypeStruct((NX, NZ, NB, ROWS, BLK), jnp.float32),
+        in_specs=[vmem, vmem],
+        out_specs=vmem,
+        compiler_params=params(),
+        name="gram_partial",
+    )(tokens, activations)
+
+
+def sum_x_kernel(first_ref, f_ref, g_ref, o_ref):
     lane = lax.broadcasted_iota(jnp.int32, (ROWS, BLK), 1)
     row = lax.broadcasted_iota(jnp.int32, (ROWS, BLK), 0)
     on_diag = lane == row + first_ref[0]
@@ -55,60 +76,38 @@
         tile = f_ref[j, :, c * BLK : (c + 1) * BLK]
         for i in range(NZ):
             o_ref[i, p] = tile
-    live = jnp.where(tok_ref[...] != PAD, 1.0, 0.0).astype(jnp.bfloat16)
-    for b in range(NB):
-        x = a_ref[:, b * BLK : (b + 1) * BLK]
-        g = jnp.dot(x.T * live, x, preferred_element_type=jnp.float32)
-        for d in range(DP):
-            o_ref[d % NZ, NP + (d // NZ) * NB + b] = g[d * ROWS : (d + 1) * ROWS]
-
-
-def pack(first, factor, tokens, activations):
-    vmem = pl.BlockSpec(memory_space=pltpu.VMEM)
-    return pl.pallas_call(
-        pack_kernel,
-        out_shape=jax.ShapeDtypeStruct((NZ, NP + NX * NB, ROWS, BLK), jnp.float32),
-        in_specs=[pl.BlockSpec(memory_space=pltpu.SMEM), vmem, vmem, vmem],
+    for i in range(NZ):
+        total = g_ref[0, i]
+        for x in range(1, NX):
+            total = total + g_ref[x, i]
+        o_ref[i, NP:] = total
+
+
+def sum_x(first, factor, received):
+    vmem = pl.BlockSpec(memory_space=pltpu.VMEM)
+    return pl.pallas_call(
+        sum_x_kernel,
+        out_shape=jax.ShapeDtypeStruct((NZ, NP + NB, ROWS, BLK), jnp.float32),
+        in_specs=[pl.BlockSpec(memory_space=pltpu.SMEM), vmem, vmem],
         out_specs=vmem,
         compiler_params=params(),
-        name="pack",
-    )(first, factor, tokens, activations)
-
-
-def sum_z_kernel(g_ref, o_ref):
-    for x in range(NX):
-        tiles = slice(NP + x * NB, NP + (x + 1) * NB)
-        total = g_ref[0, tiles]
-        for i in range(1, NZ):
-            total = total + g_ref[i, tiles]
-        o_ref[x] = total
-
-
-def sum_z(received):
-    vmem = pl.BlockSpec(memory_space=pltpu.VMEM)
-    return pl.pallas_call(
-        sum_z_kernel,
-        out_shape=jax.ShapeDtypeStruct((NX, NB, ROWS, BLK), jnp.float32),
-        in_specs=[vmem],
-        out_specs=vmem,
-        compiler_params=params(),
-        name="sum_z",
-    )(received)
-
-
-def sum_x_kernel(g_ref, own_ref, o_ref):
-    total = g_ref[0]
-    for x in range(1, NX):
-        total = total + g_ref[x]
+        name="sum_x",
+    )(first, factor, received)
+
+
+def sum_z_kernel(g_ref, own_ref, o_ref):
+    total = g_ref[0, NP:]
+    for i in range(1, NZ):
+        total = total + g_ref[i, NP:]
     own_ref[...] = total
     for d in range(DP):
         o_ref[d] = total
 
 
-def sum_x(received):
-    vmem = pl.BlockSpec(memory_space=pltpu.VMEM)
-    return pl.pallas_call(
-        sum_x_kernel,
+def sum_z(received):
+    vmem = pl.BlockSpec(memory_space=pltpu.VMEM)
+    return pl.pallas_call(
+        sum_z_kernel,
         out_shape=(
             jax.ShapeDtypeStruct((NB, ROWS, BLK), jnp.float32),
             jax.ShapeDtypeStruct((DP, NB, ROWS, BLK), jnp.float32),
@@ -116,7 +115,7 @@
         in_specs=[vmem],
         out_specs=(vmem, vmem),
         compiler_params=params(),
-        name="sum_x",
+        name="sum_z",
     )(received)
 
 
@@ -324,12 +323,12 @@
     tokens = token_ids.reshape(1, -1)
     x = lax.axis_index("x").reshape(1).astype(jnp.int32)
     first = (lax.axis_index(dp) * ROWS).reshape(1).astype(jnp.int32)
-    packed = pack(first, inv_chol, tokens, activations)
+    partial = gram_partial(tokens, activations)
+    rows = exchange(partial, "x")
+    grams = error_grams(weight)
+    packed = sum_x(first, inv_chol, rows)
     over_z = exchange(packed, "z")
-    grams = error_grams(weight)
-    rows = sum_z(over_z)
-    rows = exchange(rows, "x")
-    own, copies = sum_x(rows)
+    own, copies = sum_z(over_z)
     gram = exchange(copies, dp)
     mine, _ = lax.optimization_barrier((over_z, copies))
     mine = mine[:, :NP]

time: 130 us -> 125 us (0.962)
  blocking collectives: 83.8 us -> 65.2 us
  waiting for transfers between devices: 0.01 us -> 6.94 us
  starting transfers between devices: 12.3 us -> 17.9 us
    all_to_all x4 -> x3, blocking collectives: 83.8 us -> 65.2 us  [exchange(): return lax.all_to_all(pieces, axes, 0, 0, tiled=False)]
    all_to_all x1 -> x2, waiting for transfers between devices: 0.01 us -> 6.94 us  [exchange(): return lax.all_to_all(pieces, axes, 0, 0, tiled=False)]
    all_to_all x1 -> x2, starting transfers between devices: 3.89 us -> 9.47 us  [exchange(): return lax.all_to_all(pieces, axes, 0, 0, tiled=False)]
  transfers between devices with their start and end apart: 4 -> 5, of which waited for: 0 -> 1; matrix products, arithmetic and copies ran while one was open for 1% -> 1% of each run, Pallas kernels for 13% -> 13%
where the time goes in v3:
time: 125 us; the launch traced here: 124 us
  blocking collectives  65.2 us (52%)
  Pallas kernels  29.8 us (24%)
  starting transfers between devices  17.9 us (14%)
  waiting for transfers between devices  6.94 us (6%)
  local copies, waits for them, and re-layouts  3.57 us (3%)
    all_to_all x3, blocking collectives, exchange(): return lax.all_to_all(pieces, axes, 0, 0, tiled=False)  65.2 us
    pallas_call x1, Pallas kernels, error_grams(): pl.pallas_call(error_kernel, out_shape=jax.ShapeDtypeStruct((NB, 4, DP, R...  10.5 us
    all_to_all x2, starting transfers between devices, exchange(): return lax.all_to_all(pieces, axes, 0, 0, tiled=False)  9.47 us
    ppermute x3, starting transfers between devices, shift_x(): return lax.ppermute(piece, 'x', [(i, (i + by) % NX) for i in range(NX)])  8.41 us
    pallas_call x1, Pallas kernels, quantize(): pl.pallas_call(quant_kernel, out_shape=jax.ShapeDtypeStruct((rows, PANEL)...  6.97 us
    all_to_all x2, waiting for transfers between devices, exchange(): return lax.all_to_all(pieces, axes, 0, 0, tiled=False)  6.94 us
    pallas_call x1, Pallas kernels, scores(): pl.pallas_call(score_kernel, out_shape=jax.ShapeDtypeStruct((DP, 1, BLK),...  2.83 us
    pallas_call x1, Pallas kernels, gram_partial(): pl.pallas_call(gram_kernel, out_shape=jax.ShapeDtypeStruct((NX, NZ, NB, R...  2.53 us
  transfers between devices with their start and end apart: 5, of which 1 were waited for; matrix products, arithmetic and copies ran while one was open for 1% of the time, Pallas kernels for 13%

profile of v3, /device:TPU:1, one launch (start us, length us, event | category | flops | bytes accessed | tf_op | source)
XLA Modules:
  0.0 124.1 jit_solution(10656240254823934241)
XLA Ops:
  0.6 2.5 %gram_partial.1 = f32[4,8,8,4,128]{4,3,2,1,0:T(4,128)} custom-call(s32[1,512]{1,0:T(1,128)} %bitcast.4, bf16[512,1024]{1,0:T(8,128)(2,1)} %a_ref.1), custom_call_target="tpu_custom_call" | custom-call | tf_op jit(solution)/shard_map/gram_partial/pallas_call | solution.py:54
  3.2 4.8 %all-to-all-start = ((f32[4,8,8,4,128]{4,3,2,1,0:T(4,128)}), f32[4,8,8,4,128]{4,3,2,1,0:T(4,128)S(1)}, u32[]{:S(2)}, u32[]{:S(2)}) async-start(f32[4,8,8,4,128]{4,3,2,1,0:T(4,128)} %gram_partial.1), calls=%async_computation | async-start | bytes 1048576 | tf_op jit(solution)/shard_map/all_to_all | solution.py:313
  8.0 6.9 %all-to-all-done.g_ref = f32[4,8,8,4,128]{4,3,2,1,0:T(4,128)S(1)} async-done(((f32[4,8,8,4,128]{4,3,2,1,0:T(4,128)}), f32[4,8,8,4,128]{4,3,2,1,0:T(4,128)S(1)}, u32[]{:S(2)}, u32[]{:S(2)}) %all-to-all-start) | async-done | bytes 524320 | tf_op jit(solution)/shard_map/all_to_all | solution.py:313
  14.9 0.0 copy-start
  14.9 0.8 copy-done
  15.7 2.0 %sum_x.1 = f32[8,37,4,128]{3,2,1,0:T(4,128)} custom-call(s32[1]{0:T(128)} %bitcast.1.first_ref, f32[8,4,1024]{2,1,0:T(4,128)} %f_ref.1, f32[4,8,8,4,128]{4,3,2,1,0:T(4,128)} %copy-done), custom_call_target="tpu_custom_call" | custom-call | tf_op jit(solution)/shard_map/sum_x/pallas_call | solution.py:88
  17.8 27.3 %all_to_all.25.g_ref = f32[8,37,4,128]{3,2,1,0:T(4,128)} all-to-all(f32[8,37,4,128]{3,2,1,0:T(4,128)} %sum_x.1), channel_id=1, replica_groups=mesh['x'=4,'z'=8,'y'=8,'c'=2] {'z'}, dimensions={0} | all-to-all | bytes 1212416 | tf_op jit(solution)/shard_map/all_to_all | solution.py:313
  45.1 2.0 %sum_z.1 = (f32[8,4,128]{2,1,0:T(4,128)}, f32[32,8,4,128]{3,2,1,0:T(4,128)}) custom-call(f32[8,37,4,128]{3,2,1,0:T(4,128)} %all_to_all.25.g_ref), custom_call_target="tpu_custom_call" | custom-call | tf_op jit(solution)/shard_map/sum_z/pallas_call | solution.py:109
  47.1 4.6 %all-to-all-start.2 = ((f32[32,8,4,128]{3,2,1,0:T(4,128)}), f32[32,8,4,128]{3,2,1,0:T(4,128)S(1)}, u32[]{:S(2)}, u32[]{:S(2)}) async-start(f32[32,8,4,128]{3,2,1,0:T(4,128)} %get-tuple-element.9), calls=%async_computation.2 | async-start | bytes 1048576 | tf_op jit(solution)/shard_map/all_to_all | solution.py:313
  51.7 1.1 slice.3.own_ref
  52.8 0.0 copy-start.2
  52.8 3.1 %collective-permute-start = (f32[8,29,4,128]{3,2,1,0:T(4,128)S(1)}, f32[8,29,4,128]{3,2,1,0:T(4,128)S(1)}, u32[]{:S(2)}, u32[]{:S(2)}) collective-permute-start(f32[8,29,4,128]{3,2,1,0:T(4,128)S(1)} %slice.3.own_ref), channel_id=1, source_target_pairs={{0,128},{128,256},{256,384},{384,0},{1,129},{129,257},{257,385},{3... | collective-permute-start | bytes 1425416 | tf_op jit(solution)/shard_map/ppermute | solution.py:317
  55.9 10.5 %error_grams.1.s_ref = f32[8,4,32,4,128]{4,3,2,1,0:T(4,128)} custom-call(bf16[512,1024]{1,0:T(8,128)(2,1)} %w_ref.3), custom_call_target="tpu_custom_call" | custom-call | tf_op jit(solution)/shard_map/error_grams/pallas_call | solution.py:137
  66.4 3.3 %collective-permute-start.1 = (f32[8,29,4,128]{3,2,1,0:T(4,128)S(1)}, f32[8,29,4,128]{3,2,1,0:T(4,128)S(1)}, u32[]{:S(2)}, u32[]{:S(2)}) collective-permute-start(f32[8,29,4,128]{3,2,1,0:T(4,128)S(1)} %slice.3.own_ref), channel_id=1, source_target_pairs={{0,384},{128,0},{256,128},{384,256},{1,385},{129,1},{257,129},{385... | collective-permute-start | bytes 1425416 | tf_op jit(solution)/shard_map/ppermute | solution.py:317
  69.7 0.0 all-to-all-done.2.g_ref
  69.8 0.0 copy-start.1
  69.8 0.8 copy-done.1
  70.5 2.8 %scores.1 = f32[32,1,128]{2,1,0:T(1,128)} custom-call(s32[1,512]{1,0:T(1,128)} %bitcast.5, f32[32,8,4,128]{3,2,1,0:T(4,128)} %copy-done.1, f32[8,4,32,4,128]{4,3,2,1,0:T(4,128)} %error_grams.1.s_ref), custom_call_target="tpu_custom_call" | custom-call | tf_op jit(solution)/shard_map/scores/pallas_call | solution.py:165
  73.4 0.0 copy-done.2
  73.4 0.0 collective-permute-done.left_ref
  73.4 1.9 %collective-permute-start.2 = (f32[8,29,4,128]{3,2,1,0:T(4,128)S(1)}, f32[8,29,4,128]{3,2,1,0:T(4,128)S(1)}, u32[]{:S(2)}, u32[]{:S(2)}) collective-permute-start(f32[8,29,4,128]{3,2,1,0:T(4,128)S(1)} %collective-permute-done.left_ref), channel_id=1, source_target_pairs={{0,128},{128,256},{256,384},{384,0},{1,129},{129,257},{257,385},{3... | collective-permute-start | bytes 1425416 | tf_op jit(solution)/shard_map/ppermute | solution.py:317
  75.3 17.9 %all_to_all.26.r_ref = f32[32,1,128]{2,1,0:T(1,128)} all-to-all(f32[32,1,128]{2,1,0:T(1,128)} %scores.1), channel_id=1, replica_groups=mesh['x'=4,'z'=8,'y'=8,'c'=2] {'x','z'}, dimensions={0} | all-to-all | bytes 32768 | tf_op jit(solution)/shard_map/all_to_all | solution.py:313
  93.2 1.5 %totals.1 = (f32[8,4,128]{2,1,0:T(4,128)}, f32[16,1,128]{2,1,0:T(1,128)}) custom-call(f32[32,1,128]{2,1,0:T(1,128)} %all_to_all.26.r_ref, f32[8,4,128]{2,1,0:T(4,128)} %get-tuple-element.12.own_ref), custom_call_target="tpu_custom_call" | custom-call | tf_op jit(solution)/shard_map/totals/pallas_call | solution.py:193
  94.7 20.0 %all_to_all.27.r_ref = f32[16,1,128]{2,1,0:T(1,128)} all-to-all(f32[16,1,128]{2,1,0:T(1,128)} %get-tuple-element.14), channel_id=1, replica_groups=mesh['x'=4,'z'=8,'y'=8,'c'=2] {'y','c'}, dimensions={0} | all-to-all | bytes 16384 | tf_op jit(solution)/shard_map/all_to_all | solution.py:313
  114.7 1.4 %spread.1 = f32[4,128]{1,0:T(4,128)} custom-call(f32[16,1,128]{2,1,0:T(1,128)} %all_to_all.27.r_ref), custom_call_target="tpu_custom_call" | custom-call | tf_op jit(solution)/shard_map/spread/pallas_call | solution.py:225
  116.2 0.0 collective-permute-done.1.right_ref
  116.2 0.0 collective-permute-done.2.far_ref
  116.2 0.0 copy-start.5
  116.2 0.0 copy-done.3
  116.2 0.7 copy-done.4
  116.9 0.2 copy-done.5
  117.1 7.0 %quantize.1 = bf16[512,1024]{1,0:T(8,128)(2,1)} custom-call(s32[8]{0:T(128)} %bits_ref.1, s32[1]{0:T(128)} %bitcast.x_ref, bf16[512,1024]{1,0:T(8,128)(2,1)} %w_ref.3, f32[8,29,4,128]{3,2,1,0:T(4,128)} %copy-done.2, f32[8,29,4,128]{3,2,1,0:T(4,128)} %copy-done.3, f32[8,29,4,128]{3,2,1,0:T(4,128)} %copy-done.4, f32[8,29,4,128]{3,2,1,0:T(4,128)} %copy-done.5), custom_call_target="tpu_custom_call" | custom-call | tf_op jit(solution)/shard_map/quantize/pallas_call | solution.py:293
  (2 shorter events, 0.0 us)
Async XLA Ops:
  3.2 11.8 %all-to-all-start = ((f32[4,8,8,4,128]{4,3,2,1,0:T(4,128)}), f32[4,8,8,4,128]{4,3,2,1,0:T(4,128)S(1)}, u32[]{:S(2)}, u32[]{:S(2)}) async-start(f32[4,8,8,4,128]{4,3,2,1,0:T(4,128)} %gram_partial.1), calls=%async_computation | async-start | bytes 1048576 | tf_op jit(solution)/shard_map/all_to_all | solution.py:313
  14.9 0.8 copy-start
  47.1 22.7 %all-to-all-start.2 = ((f32[32,8,4,128]{3,2,1,0:T(4,128)}), f32[32,8,4,128]{3,2,1,0:T(4,128)S(1)}, u32[]{:S(2)}, u32[]{:S(2)}) async-start(f32[32,8,4,128]{3,2,1,0:T(4,128)} %get-tuple-element.9), calls=%async_computation.2 | async-start | bytes 1048576 | tf_op jit(solution)/shard_map/all_to_all | solution.py:313
  52.8 20.6 %copy-start.2 = (f32[8,29,4,128]{3,2,1,0:T(4,128)}, f32[8,29,4,128]{3,2,1,0:T(4,128)S(1)}, u32[]{:S(2)}) copy-start(f32[8,29,4,128]{3,2,1,0:T(4,128)S(1)} %slice.3.own_ref) | copy-start | bytes 1425412
  52.8 20.6 %collective-permute-start = (f32[8,29,4,128]{3,2,1,0:T(4,128)S(1)}, f32[8,29,4,128]{3,2,1,0:T(4,128)S(1)}, u32[]{:S(2)}, u32[]{:S(2)}) collective-permute-start(f32[8,29,4,128]{3,2,1,0:T(4,128)S(1)} %slice.3.own_ref), channel_id=1, source_target_pairs={{0,128},{128,256},{256,384},{384,0},{1,129},{129,257},{257,385},{3... | collective-permute-start | bytes 1425416 | tf_op jit(solution)/shard_map/ppermute | solution.py:317
  66.4 49.8 %collective-permute-start.1 = (f32[8,29,4,128]{3,2,1,0:T(4,128)S(1)}, f32[8,29,4,128]{3,2,1,0:T(4,128)S(1)}, u32[]{:S(2)}, u32[]{:S(2)}) collective-permute-start(f32[8,29,4,128]{3,2,1,0:T(4,128)S(1)} %slice.3.own_ref), channel_id=1, source_target_pairs={{0,384},{128,0},{256,128},{384,256},{1,385},{129,1},{257,129},{385... | collective-permute-start | bytes 1425416 | tf_op jit(solution)/shard_map/ppermute | solution.py:317
  69.8 0.8 copy-start.1
  73.4 42.8 %copy-start.3 = (f32[8,29,4,128]{3,2,1,0:T(4,128)}, f32[8,29,4,128]{3,2,1,0:T(4,128)S(1)}, u32[]{:S(2)}) copy-start(f32[8,29,4,128]{3,2,1,0:T(4,128)S(1)} %collective-permute-done.left_ref) | copy-start | bytes 1425412
  73.4 42.8 %collective-permute-start.2 = (f32[8,29,4,128]{3,2,1,0:T(4,128)S(1)}, f32[8,29,4,128]{3,2,1,0:T(4,128)S(1)}, u32[]{:S(2)}, u32[]{:S(2)}) collective-permute-start(f32[8,29,4,128]{3,2,1,0:T(4,128)S(1)} %collective-permute-done.left_ref), channel_id=1, source_target_pairs={{0,128},{128,256},{256,384},{384,0},{1,129},{129,257},{257,385},{3... | collective-permute-start | bytes 1425416 | tf_op jit(solution)/shard_map/ppermute | solution.py:317
  116.2 0.8 copy-start.4
  116.2 0.9 copy-start.5

commit v4 on v3

--- a/solution.py
+++ b/solution.py
@@ -53,7 +53,7 @@
     vmem = pl.BlockSpec(memory_space=pltpu.VMEM)
     return pl.pallas_call(
         gram_kernel,
-        out_shape=jax.ShapeDtypeStruct((NX, NZ, NB, ROWS, BLK), jnp.float32),
+        out_shape=pltpu.VMEM((NX, NZ, NB, ROWS, BLK), jnp.float32),
         in_specs=[vmem, vmem],
         out_specs=vmem,
         compiler_params=params(),
@@ -317,6 +317,10 @@
     return lax.ppermute(piece, "x", [(i, (i + by) % NX) for i in range(NX)])
 
 
+def near(array):
+    return pltpu.with_memory_space_constraint(array, pltpu.VMEM)
+
+
 def per_device(activations, token_ids, weight, inv_chol, bit_widths):
     dp = ("x", "z")
     tensor = ("y", "c")
@@ -326,22 +330,22 @@
     partial = gram_partial(tokens, activations)
     rows = exchange(partial, "x")
     grams = error_grams(weight)
-    packed = sum_x(first, inv_chol, rows)
+    packed = sum_x(first, inv_chol, near(rows))
     over_z = exchange(packed, "z")
-    own, copies = sum_z(over_z)
+    own, copies = sum_z(near(over_z))
     gram = exchange(copies, dp)
     mine, _ = lax.optimization_barrier((over_z, copies))
     mine = mine[:, :NP]
     left = shift_x(mine, 1)
     right = shift_x(mine, -1)
-    row = scores(tokens, gram, grams)
+    row = scores(tokens, near(gram), near(grams))
     left_late, _ = lax.optimization_barrier((left, row))
     row = exchange(row, dp)
     far = shift_x(left_late, 1)
-    gram_out, row = totals(row, own)
+    gram_out, row = totals(near(row), near(own))
     rows = exchange(row, tensor)
-    quantized = quantize(bit_widths, x, weight, (mine, left, right, far))
-    block_errors = spread(rows).T
+    quantized = quantize(bit_widths, x, weight, tuple(map(near, (mine, left, right, far))))
+    block_errors = spread(near(rows)).T
     return quantized, gram_out, block_errors
 
 

time: 125 us -> 118 us (0.944)
  Pallas kernels: 29.8 us -> 25.4 us
  local copies, waits for them, and re-layouts: 3.57 us -> 1.62 us
    unnamed x12 -> x4, local copies, waits for them, and re-layouts: 2.51 us -> 1.59 us
  transfers between devices with their start and end apart: 5 -> 5, of which waited for: 1 -> 1; matrix products, arithmetic and copies ran while one was open for 1% -> 0% of each run, Pallas kernels for 13% -> 12%
where the time goes in v4:
time: 118 us
  blocking collectives  65.7 us (56%)
  Pallas kernels  25.4 us (22%)
  starting transfers between devices  17.4 us (15%)
  waiting for transfers between devices  6.94 us (6%)
  local copies, waits for them, and re-layouts  1.62 us (1%)
    all_to_all x3, blocking collectives, exchange(): return lax.all_to_all(pieces, axes, 0, 0, tiled=False)  65.7 us
    pallas_call x1, Pallas kernels, error_grams(): pl.pallas_call(error_kernel, out_shape=jax.ShapeDtypeStruct((NB, 4, DP, R...  10.5 us
    all_to_all x2, starting transfers between devices, exchange(): return lax.all_to_all(pieces, axes, 0, 0, tiled=False)  8.99 us
    ppermute x3, starting transfers between devices, shift_x(): return lax.ppermute(piece, 'x', [(i, (i + by) % NX) for i in range(NX)])  8.4 us
    all_to_all x2, waiting for transfers between devices, exchange(): return lax.all_to_all(pieces, axes, 0, 0, tiled=False)  6.94 us
    pallas_call x1, Pallas kernels, quantize(): pl.pallas_call(quant_kernel, out_shape=jax.ShapeDtypeStruct((rows, PANEL)...  6.41 us
    pallas_call x1, Pallas kernels, gram_partial(): pl.pallas_call(gram_kernel, out_shape=pltpu.VMEM((NX, NZ, NB, ROWS, BLK),...  2.53 us
  transfers between devices with their start and end apart: 5, of which 1 were waited for; matrix products, arithmetic and copies ran while one was open for 0% of the time, Pallas kernels for 12%

profile of v4, /device:TPU:1, one launch (start us, length us, event | category | flops | bytes accessed | tf_op | source)
XLA Modules:
  0.0 117.7 jit_solution(11580415837411461947)
XLA Ops:
  0.6 2.5 %gram_partial.1 = f32[4,8,8,4,128]{4,3,2,1,0:T(4,128)} custom-call(s32[1,512]{1,0:T(1,128)} %bitcast.4, bf16[512,1024]{1,0:T(8,128)(2,1)} %a_ref.1), custom_call_target="tpu_custom_call" | custom-call | tf_op jit(solution)/shard_map/gram_partial/pallas_call | solution.py:54
  3.2 4.8 %all-to-all-start = ((f32[4,8,8,4,128]{4,3,2,1,0:T(4,128)}), f32[4,8,8,4,128]{4,3,2,1,0:T(4,128)S(1)}, u32[]{:S(2)}, u32[]{:S(2)}) async-start(f32[4,8,8,4,128]{4,3,2,1,0:T(4,128)} %gram_partial.1), calls=%async_computation | async-start | bytes 1048576 | tf_op jit(solution)/shard_map/all_to_all | solution.py:313
  8.0 6.9 %all-to-all-done.g_ref = f32[4,8,8,4,128]{4,3,2,1,0:T(4,128)S(1)} async-done(((f32[4,8,8,4,128]{4,3,2,1,0:T(4,128)}), f32[4,8,8,4,128]{4,3,2,1,0:T(4,128)S(1)}, u32[]{:S(2)}, u32[]{:S(2)}) %all-to-all-start) | async-done | bytes 524320 | tf_op jit(solution)/shard_map/all_to_all | solution.py:313
  14.9 1.8 %sum_x.1 = f32[8,37,4,128]{3,2,1,0:T(4,128)} custom-call(s32[1]{0:T(128)} %bitcast.1.first_ref, f32[8,4,1024]{2,1,0:T(4,128)} %f_ref.1, f32[4,8,8,4,128]{4,3,2,1,0:T(4,128)S(1)} %all-to-all-done.g_ref), custom_call_target="tpu_custom_call" | custom-call | tf_op jit(solution)/shard_map/sum_x/pallas_call | solution.py:88
  16.8 27.4 %all_to_all.25.g_ref = f32[8,37,4,128]{3,2,1,0:T(4,128)S(1)} all-to-all(f32[8,37,4,128]{3,2,1,0:T(4,128)} %sum_x.1), channel_id=1, replica_groups=mesh['x'=4,'z'=8,'y'=8,'c'=2] {'z'}, dimensions={0} | all-to-all | bytes 1212416 | tf_op jit(solution)/shard_map/all_to_all | solution.py:313
  44.2 0.9 sum_z.1
  45.1 4.2 %all-to-all-start.2 = ((f32[32,8,4,128]{3,2,1,0:T(4,128)}), f32[32,8,4,128]{3,2,1,0:T(4,128)S(1)}, u32[]{:S(2)}, u32[]{:S(2)}) async-start(f32[32,8,4,128]{3,2,1,0:T(4,128)} %get-tuple-element.9), calls=%async_computation.2 | async-start | bytes 1048576 | tf_op jit(solution)/shard_map/all_to_all | solution.py:313
  49.3 3.1 %collective-permute-start = (f32[8,29,4,128]{3,2,1,0:T(4,128)S(1)}, f32[8,29,4,128]{3,2,1,0:T(4,128)S(1)}, u32[]{:S(2)}, u32[]{:S(2)}) collective-permute-start(f32[8,29,4,128]{3,2,1,0:T(4,128)S(1)} %slice.3.own_ref), channel_id=1, source_target_pairs={{0,128},{128,256},{256,384},{384,0},{1,129},{129,257},{257,385},{3... | collective-permute-start | bytes 1425416 | tf_op jit(solution)/shard_map/ppermute | solution.py:317
  52.5 0.0 copy-start.1
  52.5 10.5 %error_grams.1.s_ref = f32[8,4,32,4,128]{4,3,2,1,0:T(4,128)} custom-call(bf16[512,1024]{1,0:T(8,128)(2,1)} %w_ref.3), custom_call_target="tpu_custom_call" | custom-call | tf_op jit(solution)/shard_map/error_grams/pallas_call | solution.py:137
  63.0 3.3 %collective-permute-start.1 = (f32[8,29,4,128]{3,2,1,0:T(4,128)S(1)}, f32[8,29,4,128]{3,2,1,0:T(4,128)S(1)}, u32[]{:S(2)}, u32[]{:S(2)}) collective-permute-start(f32[8,29,4,128]{3,2,1,0:T(4,128)S(1)} %slice.3.own_ref), channel_id=1, source_target_pairs={{0,384},{128,0},{256,128},{384,256},{1,385},{129,1},{257,129},{385... | collective-permute-start | bytes 1425416 | tf_op jit(solution)/shard_map/ppermute | solution.py:317
  66.3 0.0 all-to-all-done.2.g_ref
  66.3 0.0 copy-start
  66.3 1.6 %copy-done = f32[8,4,32,4,128]{4,3,2,1,0:T(4,128)S(1)} copy-done((f32[8,4,32,4,128]{4,3,2,1,0:T(4,128)S(1)}, f32[8,4,32,4,128]{4,3,2,1,0:T(4,128)}, u32[]{:S(2)}) %copy-start) | copy-done | bytes 2097176
  67.9 1.7 %scores.1 = f32[32,1,128]{2,1,0:T(1,128)} custom-call(s32[1,512]{1,0:T(1,128)} %bitcast.5, f32[32,8,4,128]{3,2,1,0:T(4,128)S(1)} %all-to-all-done.2.g_ref, f32[8,4,32,4,128]{4,3,2,1,0:T(4,128)S(1)} %copy-done), custom_call_target="tpu_custom_call" | custom-call | tf_op jit(solution)/shard_map/scores/pallas_call | solution.py:165
  69.6 0.0 collective-permute-done.left_ref
  69.6 1.9 %collective-permute-start.2 = (f32[8,29,4,128]{3,2,1,0:T(4,128)S(1)}, f32[8,29,4,128]{3,2,1,0:T(4,128)S(1)}, u32[]{:S(2)}, u32[]{:S(2)}) collective-permute-start(f32[8,29,4,128]{3,2,1,0:T(4,128)S(1)} %collective-permute-done.left_ref), channel_id=1, source_target_pairs={{0,128},{128,256},{256,384},{384,0},{1,129},{129,257},{257,385},{3... | collective-permute-start | bytes 1425416 | tf_op jit(solution)/shard_map/ppermute | solution.py:317
  71.6 17.8 %all_to_all.26.r_ref = f32[32,1,128]{2,1,0:T(1,128)S(1)} all-to-all(f32[32,1,128]{2,1,0:T(1,128)} %scores.1), channel_id=1, replica_groups=mesh['x'=4,'z'=8,'y'=8,'c'=2] {'x','z'}, dimensions={0} | all-to-all | bytes 32768 | tf_op jit(solution)/shard_map/all_to_all | solution.py:313
  89.3 0.0 copy-done.1
  89.4 0.8 totals.1
  90.1 20.5 %all_to_all.27.r_ref = f32[16,1,128]{2,1,0:T(1,128)S(1)} all-to-all(f32[16,1,128]{2,1,0:T(1,128)} %get-tuple-element.14), channel_id=1, replica_groups=mesh['x'=4,'z'=8,'y'=8,'c'=2] {'y','c'}, dimensions={0} | all-to-all | bytes 16384 | tf_op jit(solution)/shard_map/all_to_all | solution.py:313
  110.6 0.7 spread.1
  111.3 0.0 collective-permute-done.1.right_ref
  111.3 0.0 collective-permute-done.2.far_ref
  111.3 6.4 %quantize.1 = bf16[512,1024]{1,0:T(8,128)(2,1)} custom-call(s32[8]{0:T(128)} %bits_ref.1, s32[1]{0:T(128)} %bitcast.x_ref, bf16[512,1024]{1,0:T(8,128)(2,1)} %w_ref.3, f32[8,29,4,128]{3,2,1,0:T(4,128)S(1)} %slice.3.own_ref, f32[8,29,4,128]{3,2,1,0:T(4,128)S(1)} %collective-permute-done.left_ref, f32[8,29,4,128]{3,2,1,0:T(4,128)S(1)} %collective-permute-done.1.right_ref, ...), custom_call_target="tpu_custom_call" | custom-call | tf_op jit(solution)/shard_map/quantize/pallas_call | solution.py:293
  (1 shorter events, 0.0 us)
Async XLA Ops:
  3.2 11.8 %all-to-all-start = ((f32[4,8,8,4,128]{4,3,2,1,0:T(4,128)}), f32[4,8,8,4,128]{4,3,2,1,0:T(4,128)S(1)}, u32[]{:S(2)}, u32[]{:S(2)}) async-start(f32[4,8,8,4,128]{4,3,2,1,0:T(4,128)} %gram_partial.1), calls=%async_computation | async-start | bytes 1048576 | tf_op jit(solution)/shard_map/all_to_all | solution.py:313
  45.1 21.2 %all-to-all-start.2 = ((f32[32,8,4,128]{3,2,1,0:T(4,128)}), f32[32,8,4,128]{3,2,1,0:T(4,128)S(1)}, u32[]{:S(2)}, u32[]{:S(2)}) async-start(f32[32,8,4,128]{3,2,1,0:T(4,128)} %get-tuple-element.9), calls=%async_computation.2 | async-start | bytes 1048576 | tf_op jit(solution)/shard_map/all_to_all | solution.py:313
  49.3 20.3 %collective-permute-start = (f32[8,29,4,128]{3,2,1,0:T(4,128)S(1)}, f32[8,29,4,128]{3,2,1,0:T(4,128)S(1)}, u32[]{:S(2)}, u32[]{:S(2)}) collective-permute-start(f32[8,29,4,128]{3,2,1,0:T(4,128)S(1)} %slice.3.own_ref), channel_id=1, source_target_pairs={{0,128},{128,256},{256,384},{384,0},{1,129},{129,257},{257,385},{3... | collective-permute-start | bytes 1425416 | tf_op jit(solution)/shard_map/ppermute | solution.py:317
  52.5 36.9 %copy-start.1 = (f32[8,4,128]{2,1,0:T(4,128)S(1)}, f32[8,4,128]{2,1,0:T(4,128)}, u32[]{:S(2)}) copy-start(f32[8,4,128]{2,1,0:T(4,128)} %get-tuple-element.12.own_ref) | copy-start | bytes 49156
  63.0 48.4 %collective-permute-start.1 = (f32[8,29,4,128]{3,2,1,0:T(4,128)S(1)}, f32[8,29,4,128]{3,2,1,0:T(4,128)S(1)}, u32[]{:S(2)}, u32[]{:S(2)}) collective-permute-start(f32[8,29,4,128]{3,2,1,0:T(4,128)S(1)} %slice.3.own_ref), channel_id=1, source_target_pairs={{0,384},{128,0},{256,128},{384,256},{1,385},{129,1},{257,129},{385... | collective-permute-start | bytes 1425416 | tf_op jit(solution)/shard_map/ppermute | solution.py:317
  66.3 1.6 %copy-start = (f32[8,4,32,4,128]{4,3,2,1,0:T(4,128)S(1)}, f32[8,4,32,4,128]{4,3,2,1,0:T(4,128)}, u32[]{:S(2)}) copy-start(f32[8,4,32,4,128]{4,3,2,1,0:T(4,128)} %error_grams.1.s_ref) | copy-start | bytes 6291460
  69.6 41.7 %collective-permute-start.2 = (f32[8,29,4,128]{3,2,1,0:T(4,128)S(1)}, f32[8,29,4,128]{3,2,1,0:T(4,128)S(1)}, u32[]{:S(2)}, u32[]{:S(2)}) collective-permute-start(f32[8,29,4,128]{3,2,1,0:T(4,128)S(1)} %collective-permute-done.left_ref), channel_id=1, source_target_pairs={{0,128},{128,256},{256,384},{384,0},{1,129},{129,257},{257,385},{3... | collective-permute-start | bytes 1425416 | tf_op jit(solution)/shard_map/ppermute | solution.py:317

commit v5 on v4

--- a/solution.py
+++ b/solution.py
@@ -12,8 +12,11 @@
 DP = 32
 ROWS = BLK // DP
 NX, NZ, NY, NC = 4, 8, 8, 2
+NT = NY * NC
 PAIRS = [(j, c) for j in range(NB) for c in range(j + 1, NB)]
 NP = len(PAIRS) + 1
+HB = NB // 2
+GT = HB + 1
 PAD = 128004
 LEVELS = (2.0, 4.0, 8.0, 128.0)
 
@@ -42,18 +45,31 @@
 
 def gram_kernel(tok_ref, a_ref, o_ref):
     live = jnp.where(tok_ref[...] != PAD, 1.0, 0.0).astype(jnp.bfloat16)
-    for b in range(NB):
+    row = lax.broadcasted_iota(jnp.int32, (BLK, BLK), 0)
+    col = lax.broadcasted_iota(jnp.int32, (BLK, BLK), 1)
+    diag = jnp.zeros((BLK, BLK), jnp.float32)
+
+    def gram(b):
         x = a_ref[:, b * BLK : (b + 1) * BLK]
-        g = jnp.dot(x.T * live, x, preferred_element_type=jnp.float32)
+        return jnp.dot(x.T * live, x, preferred_element_type=jnp.float32)
+
+    def put(g, tile):
         for d in range(DP):
-            o_ref[d // NZ, d % NZ, b] = g[d * ROWS : (d + 1) * ROWS]
+            o_ref[d // NZ, d % NZ, tile] = g[d * ROWS : (d + 1) * ROWS]
+
+    for b in range(HB):
+        lower = gram(b + HB)
+        put(jnp.where(col >= row, gram(b), lower), b)
+        value = jnp.sum(jnp.where(col == row, lower, 0.0), axis=1, keepdims=True)
+        diag = jnp.where(col == b + HB, value, diag)
+    put(diag, HB)
 
 
 def gram_partial(tokens, activations):
     vmem = pl.BlockSpec(memory_space=pltpu.VMEM)
     return pl.pallas_call(
         gram_kernel,
-        out_shape=pltpu.VMEM((NX, NZ, NB, ROWS, BLK), jnp.float32),
+        out_shape=pltpu.VMEM((NX, NZ, GT, ROWS, BLK), jnp.float32),
         in_specs=[vmem, vmem],
         out_specs=vmem,
         compiler_params=params(),
@@ -87,7 +103,7 @@
     vmem = pl.BlockSpec(memory_space=pltpu.VMEM)
     return pl.pallas_call(
         sum_x_kernel,
-        out_shape=jax.ShapeDtypeStruct((NZ, NP + NB, ROWS, BLK), jnp.float32),
+        out_shape=jax.ShapeDtypeStruct((NZ, NP + GT, ROWS, BLK), jnp.float32),
         in_specs=[pl.BlockSpec(memory_space=pltpu.SMEM), vmem, vmem],
         out_specs=vmem,
         compiler_params=params(),
@@ -109,8 +125,8 @@
     return pl.pallas_call(
         sum_z_kernel,
         out_shape=(
-            jax.ShapeDtypeStruct((NB, ROWS, BLK), jnp.float32),
-            jax.ShapeDtypeStruct((DP, NB, ROWS, BLK), jnp.float32),
+            jax.ShapeDtypeStruct((GT, ROWS, BLK), jnp.float32),
+            jax.ShapeDtypeStruct((DP, GT, ROWS, BLK), jnp.float32),
         ),
         in_specs=[vmem],
         out_specs=(vmem, vmem),
@@ -119,7 +135,13 @@
     )(received)
 
 
-def error_kernel(w_ref, o_ref):
+def error_kernel(w_ref, o_ref, d_ref):
+    b = pl.program_id(0)
+    row = lax.broadcasted_iota(jnp.int32, (BLK, BLK), 0)
+    col = lax.broadcasted_iota(jnp.int32, (BLK, BLK), 1)
+    upper = jnp.where(col > row, 2.0, jnp.where(col == row, 1.0, 0.0))
+    lower = jnp.where(col < row, 2.0, 0.0)
+    weight = jnp.where(b < HB, upper, lower)
     w = w_ref[...].astype(jnp.float32)
     bound = jnp.max(jnp.abs(w), axis=1, keepdims=True) + 1e-6
     unit = w * (1.0 / bound)
@@ -128,109 +150,134 @@
         smooth = jnp.clip(u - sine_over_two_pi(u), -levels, levels - 1.0)
         e = (w - (bound * (1.0 / (levels - 0.5))) * smooth).astype(jnp.bfloat16)
         s = lax.dot_general(e, e, (((0,), (0,)), ((), ())), preferred_element_type=jnp.float32)
+        value = jnp.sum(jnp.where(col == row, s, 0.0), axis=1, keepdims=True)
+        diag = jnp.where((col == b) & (b >= HB), value, 0.0)
+        s = s * weight
         for d in range(DP):
-            o_ref[0, k, d] = s[d * ROWS : (d + 1) * ROWS]
+            part = slice(d * ROWS, (d + 1) * ROWS)
+            o_ref[0, k, d] = s[part]
+            before = jnp.where(b == 0, 0.0, d_ref[k, d])
+            d_ref[k, d] = before + diag[part]
 
 
 def error_grams(weight):
     rows = weight.shape[0]
     return pl.pallas_call(
         error_kernel,
-        out_shape=jax.ShapeDtypeStruct((NB, 4, DP, ROWS, BLK), jnp.float32),
+        out_shape=(
+            jax.ShapeDtypeStruct((NB, 4, DP, ROWS, BLK), jnp.float32),
+            jax.ShapeDtypeStruct((4, DP, ROWS, BLK), jnp.float32),
+        ),
         grid=(NB,),
         in_specs=[pl.BlockSpec((rows, BLK), lambda b: (0, b))],
-        out_specs=pl.BlockSpec((1, 4, DP, ROWS, BLK), lambda b: (b, 0, 0, 0, 0)),
+        out_specs=(
+            pl.BlockSpec((1, 4, DP, ROWS, BLK), lambda b: (b, 0, 0, 0, 0)),
+            pl.BlockSpec((4, DP, ROWS, BLK), lambda b: (0, 0, 0, 0)),
+        ),
         compiler_params=params("arbitrary"),
         name="error_grams",
     )(weight)
 
 
-def score_kernel(tok_ref, g_ref, s_ref, o_ref, row_ref):
+def score_kernel(tok_ref, g_ref, s_ref, d_ref, o_ref, row_ref):
     row_ref[...] = jnp.zeros((BLK, BLK), jnp.float32)
     live = jnp.where(tok_ref[...] != PAD, 1.0, 0.0)
     row_ref[4 * NB : 4 * NB + 1, :] = sum(live[:, i : i + BLK] for i in range(0, live.shape[1], BLK))
-    for b in range(NB):
-        for k in range(4):
-            acc = g_ref[0, b] * s_ref[b, k, 0]
+    diagonals = jnp.zeros((1, BLK), jnp.float32)
+    for k in range(4):
+        for b in range(NB):
+            acc = g_ref[0, b % HB] * s_ref[b, k, 0]
             for d in range(1, DP):
-                acc = acc + g_ref[d, b] * s_ref[b, k, d]
+                acc = acc + g_ref[d, b % HB] * s_ref[b, k, d]
             row_ref[k * NB + b : k * NB + b + 1, :] = jnp.sum(acc, axis=0, keepdims=True)
-    row = jnp.sum(row_ref[...].T, axis=0, keepdims=True)
-    for d in range(DP):
-        o_ref[d] = row
-
-
-def scores(tokens, gram, grams):
+        acc = g_ref[0, HB] * d_ref[k, 0]
+        for d in range(1, DP):
+            acc = acc + g_ref[d, HB] * d_ref[k, d]
+        acc = jnp.sum(acc, axis=0, keepdims=True)
+        diagonals = diagonals + (pltpu.roll(acc, k * NB, 1) if k else acc)
+    row = jnp.sum(row_ref[...].T, axis=0, keepdims=True) + diagonals
+    o_ref[...] = jnp.broadcast_to(row, o_ref.shape)
+
+
+def scores(tokens, gram, grams, diagonals):
     vmem = pl.BlockSpec(memory_space=pltpu.VMEM)
     return pl.pallas_call(
         score_kernel,
-        out_shape=jax.ShapeDtypeStruct((DP, 1, BLK), jnp.float32),
-        in_specs=[vmem] * 3,
+        out_shape=jax.ShapeDtypeStruct((DP * NT, BLK), jnp.float32),
+        in_specs=[vmem] * 4,
         out_specs=vmem,
         scratch_shapes=[pltpu.VMEM((BLK, BLK), jnp.float32)],
         compiler_params=params(),
         name="scores",
-    )(tokens, gram, grams)
-
-
-def total_kernel(r_ref, own_ref, gram_ref, o_ref):
-    row = r_ref[0]
+    )(tokens, gram, grams, diagonals)
+
+
+def rows_kernel(first_ref, g_ref, own_ref, o_ref):
+    first = first_ref[0]
+    lane = lax.broadcasted_iota(jnp.int32, (ROWS, BLK), 1)
+    mine = lax.broadcasted_iota(jnp.int32, (ROWS, BLK), 0) + first
+    pick = jnp.where(
+        lax.broadcasted_iota(jnp.int32, (8, BLK), 1) == lax.broadcasted_iota(jnp.int32, (8, BLK), 0) + first, 1.0, 0.0
+    )
+    for b in range(HB):
+        square = jnp.concatenate([g_ref[d, b] for d in range(DP)], axis=0)
+        turned = lax.dot_general(
+            pick,
+            square,
+            (((1,), (1,)), ((), ())),
+            precision=lax.Precision.HIGHEST,
+            preferred_element_type=jnp.float32,
+        )[:ROWS]
+        own = own_ref[b]
+        diag = jnp.sum(jnp.where(lane == b + HB, own_ref[HB], 0.0), axis=1, keepdims=True)
+        o_ref[b] = jnp.where(lane >= mine, own, turned)
+        o_ref[b + HB] = jnp.where(lane < mine, own, jnp.where(lane == mine, diag, turned))
+
+
+def gram_rows(first, gram, own):
+    vmem = pl.BlockSpec(memory_space=pltpu.VMEM)
+    return pl.pallas_call(
+        rows_kernel,
+        out_shape=jax.ShapeDtypeStruct((NB, ROWS, BLK), jnp.float32),
+        in_specs=[pl.BlockSpec(memory_space=pltpu.SMEM), vmem, vmem],
+        out_specs=vmem,
+        compiler_params=params(),
+        name="gram_rows",
+    )(first, gram, own)
+
+
+def finish_kernel(r_ref, rows_ref, gram_ref, o_ref):
+    total = r_ref[0:NT, :]
     for d in range(1, DP):
-        row = row + r_ref[d]
-    lane = lax.broadcasted_iota(jnp.int32, (1, BLK), 1)
-    count = jnp.sum(jnp.where(lane == 4 * NB, row, 0.0))
-    gram_ref[...] = own_ref[...] / count
-    scale = jnp.zeros((1, BLK), jnp.float32)
+        total = total + r_ref[d * NT : (d + 1) * NT, :]
+    lane = lax.broadcasted_iota(jnp.int32, (8, BLK), 1)
+    source = lax.broadcasted_iota(jnp.int32, (8, BLK), 0)
+    count = jnp.sum(jnp.where((lane == 4 * NB) & (source == 0), total[:8], 0.0))
+    gram_ref[...] = rows_ref[...] / count
+    sums = [jnp.zeros((1, BLK), jnp.float32)] * 4
+    for h in range(NT // 8):
+        skewed = pltpu.roll(total[h * 8 : (h + 1) * 8], 0, 1, stride=NB, stride_axis=0)
+        for k in range(4):
+            moved = pltpu.roll(skewed, (h * 8 * NB - k * NB) % BLK, 1)
+            kept = jnp.where(lane // NB == source + h * 8, moved, 0.0)
+            sums[k] = sums[k] + jnp.sum(kept, axis=0, keepdims=True)
     for k, levels in enumerate(LEVELS):
-        scale = jnp.where(lane // NB == k, levels * levels / (OUT * BLK), scale)
-    row = row * scale / count
-    for t in range(NY * NC):
-        o_ref[t] = row
-
-
-def totals(rows, own):
-    vmem = pl.BlockSpec(memory_space=pltpu.VMEM)
-    return pl.pallas_call(
-        total_kernel,
+        o_ref[k : k + 1, :] = sums[k] * (levels * levels / (OUT * BLK)) / count
+
+
+def finish(received, rows):
+    vmem = pl.BlockSpec(memory_space=pltpu.VMEM)
+    return pl.pallas_call(
+        finish_kernel,
         out_shape=(
             jax.ShapeDtypeStruct((NB, ROWS, BLK), jnp.float32),
-            jax.ShapeDtypeStruct((NY * NC, 1, BLK), jnp.float32),
+            jax.ShapeDtypeStruct((4, BLK), jnp.float32),
         ),
         in_specs=[vmem, vmem],
         out_specs=(vmem, vmem),
         compiler_params=params(),
-        name="totals",
-    )(rows, own)
-
-
-def spread_kernel(r_ref, o_ref, row_ref):
-    n = NY * NC
-    for t in range(n):
-        row_ref[t : t + 1, :] = r_ref[t]
-    lane = lax.broadcasted_iota(jnp.int32, (8, BLK), 1)
-    source = lax.broadcasted_iota(jnp.int32, (8, BLK), 0)
-    total = [jnp.zeros((1, BLK), jnp.float32)] * 4
-    for h in range(n // 8):
-        skewed = pltpu.roll(row_ref[h * 8 : (h + 1) * 8, :], 0, 1, stride=NB, stride_axis=0)
-        for k in range(4):
-            moved = pltpu.roll(skewed, (h * 8 * NB - k * NB) % BLK, 1)
-            kept = jnp.where(lane // NB == source + h * 8, moved, 0.0)
-            total[k] = total[k] + jnp.sum(kept, axis=0, keepdims=True)
-    for k in range(4):
-        o_ref[k : k + 1, :] = total[k]
-
-
-def spread(rows):
-    vmem = pl.BlockSpec(memory_space=pltpu.VMEM)
-    return pl.pallas_call(
-        spread_kernel,
-        out_shape=jax.ShapeDtypeStruct((4, BLK), jnp.float32),
-        in_specs=[vmem],
-        out_specs=vmem,
-        scratch_shapes=[pltpu.VMEM((NY * NC, BLK), jnp.float32)],
-        compiler_params=params(),
-        name="spread",
-    )(rows)
+        name="finish",
+    )(received, rows)
 
 
 CHUNKS = 2
@@ -329,7 +376,7 @@
     first = (lax.axis_index(dp) * ROWS).reshape(1).astype(jnp.int32)
     partial = gram_partial(tokens, activations)
     rows = exchange(partial, "x")
-    grams = error_grams(weight)
+    grams, diagonals = error_grams(weight)
     packed = sum_x(first, inv_chol, near(rows))
     over_z = exchange(packed, "z")
     own, copies = sum_z(near(over_z))
@@ -338,15 +385,14 @@
     mine = mine[:, :NP]
     left = shift_x(mine, 1)
     right = shift_x(mine, -1)
-    row = scores(tokens, near(gram), near(grams))
+    row = scores(tokens, near(gram), near(grams), near(diagonals))
     left_late, _ = lax.optimization_barrier((left, row))
-    row = exchange(row, dp)
+    row = lax.all_to_all(row, dp + tensor, 0, 0, tiled=True)
     far = shift_x(left_late, 1)
-    gram_out, row = totals(near(row), near(own))
-    rows = exchange(row, tensor)
+    rows = gram_rows(first, near(gram), near(own))
     quantized = quantize(bit_widths, x, weight, tuple(map(near, (mine, left, right, far))))
-    block_errors = spread(near(rows)).T
-    return quantized, gram_out, block_errors
+    gram_out, block_errors = finish(near(row), near(rows))
+    return quantized, gram_out, block_errors.T
 
 
 def solution(mesh):

time: 118 us -> 114 us (0.966)
  blocking collectives: 65.7 us -> 25.6 us
  starting transfers between devices: 17.4 us -> 39.4 us
  waiting for transfers between devices: 6.94 us -> 18.3 us
  Pallas kernels: 25.4 us -> 26.6 us
    all_to_all x3 -> x1, blocking collectives: 65.7 us -> 25.6 us  [exchange(): return lax.all_to_all(pieces, axes, 0, 0, tiled=False)]
    all_to_all x0 -> x1, starting transfers between devices: none -> 21.1 us  [per_device(): row = lax.all_to_all(row, dp + tensor, 0, 0, tiled=True)]
    ppermute x3, waiting for transfers between devices: 0.01 us -> 12.5 us  [shift_x(): return lax.ppermute(piece, 'x', [(i, (i + by) % NX) for i in range(NX)])]
    unnamed x4 -> x8, local copies, waits for them, and re-layouts: 1.59 us -> 2.55 us
  transfers between devices with their start and end apart: 5 -> 6, of which waited for: 1 -> 3; matrix products, arithmetic and copies ran while one was open for 0% -> 0% of each run, Pallas kernels for 12% -> 18%
where the time goes in v5:
time: 114 us; the launch traced here: 113 us
  starting transfers between devices  39.4 us (35%)
  Pallas kernels  26.6 us (23%)
  blocking collectives  25.6 us (22%)
  waiting for transfers between devices  18.3 us (16%)
  local copies, waits for them, and re-layouts  2.58 us (2%)
    all_to_all x1, blocking collectives, exchange(): return lax.all_to_all(pieces, axes, 0, 0, tiled=False)  25.6 us
    all_to_all x1, starting transfers between devices, per_device(): row = lax.all_to_all(row, dp + tensor, 0, 0, tiled=True)  21.1 us
    ppermute x3, waiting for transfers between devices, shift_x(): return lax.ppermute(piece, 'x', [(i, (i + by) % NX) for i in range(NX)])  12.5 us
    pallas_call x1, Pallas kernels, error_grams(): pl.pallas_call(error_kernel, out_shape=(jax.ShapeDtypeStruct((NB, 4, DP,...  11.2 us
    ppermute x3, starting transfers between devices, shift_x(): return lax.ppermute(piece, 'x', [(i, (i + by) % NX) for i in range(NX)])  9.54 us
    all_to_all x2, starting transfers between devices, exchange(): return lax.all_to_all(pieces, axes, 0, 0, tiled=False)  8.84 us
    pallas_call x1, Pallas kernels, quantize(): pl.pallas_call(quant_kernel, out_shape=jax.ShapeDtypeStruct((rows, PANEL)...  6.43 us
    all_to_all x2, waiting for transfers between devices, exchange(): return lax.all_to_all(pieces, axes, 0, 0, tiled=False)  5.88 us
  transfers between devices with their start and end apart: 6, of which 3 were waited for; matrix products, arithmetic and copies ran while one was open for 0% of the time, Pallas kernels for 18%

profile of v5, /device:TPU:1, one launch (start us, length us, event | category | flops | bytes accessed | tf_op | source)
XLA Modules:
  0.0 113.2 jit_solution(8894505893157690138)
XLA Ops:
  0.6 2.5 %gram_partial.1 = f32[4,8,5,4,128]{4,3,2,1,0:T(4,128)} custom-call(s32[1,512]{1,0:T(1,128)} %bitcast.10, bf16[512,1024]{1,0:T(8,128)(2,1)} %a_ref.1), custom_call_target="tpu_custom_call" | custom-call | tf_op jit(solution)/shard_map/gram_partial/pallas_call | solution.py:70
  3.1 4.8 %all-to-all-start = ((f32[4,8,5,4,128]{4,3,2,1,0:T(4,128)}), f32[4,8,5,4,128]{4,3,2,1,0:T(4,128)S(1)}, u32[]{:S(2)}, u32[]{:S(2)}) async-start(f32[4,8,5,4,128]{4,3,2,1,0:T(4,128)} %gram_partial.1), calls=%async_computation | async-start | bytes 655360 | tf_op jit(solution)/shard_map/all_to_all | solution.py:360
  8.0 5.9 %all-to-all-done.g_ref = f32[4,8,5,4,128]{4,3,2,1,0:T(4,128)S(1)} async-done(((f32[4,8,5,4,128]{4,3,2,1,0:T(4,128)}), f32[4,8,5,4,128]{4,3,2,1,0:T(4,128)S(1)}, u32[]{:S(2)}, u32[]{:S(2)}) %all-to-all-start) | async-done | bytes 327712 | tf_op jit(solution)/shard_map/all_to_all | solution.py:360
  13.9 1.8 %sum_x.1 = f32[8,34,4,128]{3,2,1,0:T(4,128)} custom-call(s32[1]{0:T(128)} %bitcast.1.first_ref, f32[8,4,1024]{2,1,0:T(4,128)} %f_ref.1, f32[4,8,5,4,128]{4,3,2,1,0:T(4,128)S(1)} %all-to-all-done.g_ref), custom_call_target="tpu_custom_call" | custom-call | tf_op jit(solution)/shard_map/sum_x/pallas_call | solution.py:104
  15.6 25.6 %all_to_all.26.g_ref = f32[8,34,4,128]{3,2,1,0:T(4,128)S(1)} all-to-all(f32[8,34,4,128]{3,2,1,0:T(4,128)} %sum_x.1), channel_id=1, replica_groups=mesh['x'=4,'z'=8,'y'=8,'c'=2] {'z'}, dimensions={0} | all-to-all | bytes 1114112 | tf_op jit(solution)/shard_map/all_to_all | solution.py:360
  41.3 0.8 sum_z.1
  42.0 4.0 %all-to-all-start.2 = ((f32[32,5,4,128]{3,2,1,0:T(4,128)}), f32[32,5,4,128]{3,2,1,0:T(4,128)S(1)}, u32[]{:S(2)}, u32[]{:S(2)}) async-start(f32[32,5,4,128]{3,2,1,0:T(4,128)} %get-tuple-element.11), calls=%async_computation.2 | async-start | bytes 655360 | tf_op jit(solution)/shard_map/all_to_all | solution.py:360
  46.1 0.0 copy-start.3
  46.1 3.1 %collective-permute-start = (f32[8,29,4,128]{3,2,1,0:T(4,128)S(1)}, f32[8,29,4,128]{3,2,1,0:T(4,128)S(1)}, u32[]{:S(2)}, u32[]{:S(2)}) collective-permute-start(f32[8,29,4,128]{3,2,1,0:T(4,128)S(1)} %slice.3.own_ref), channel_id=1, source_target_pairs={{0,128},{128,256},{256,384},{384,0},{1,129},{129,257},{257,385},{3... | collective-permute-start | bytes 1425416 | tf_op jit(solution)/shard_map/ppermute | solution.py:364
  49.2 11.2 %error_grams.1 = (f32[8,4,32,4,128]{4,3,2,1,0:T(4,128)}, f32[4,32,4,128]{3,2,1,0:T(4,128)}) custom-call(bf16[512,1024]{1,0:T(8,128)(2,1)} %w_ref.3), custom_call_target="tpu_custom_call" | custom-call | tf_op jit(solution)/shard_map/error_grams/pallas_call | solution.py:165
  60.4 0.0 all-to-all-done.2.g_ref
  60.4 0.0 copy-start
  60.4 1.6 %copy-done = f32[8,4,32,4,128]{4,3,2,1,0:T(4,128)S(1)} copy-done((f32[8,4,32,4,128]{4,3,2,1,0:T(4,128)S(1)}, f32[8,4,32,4,128]{4,3,2,1,0:T(4,128)}, u32[]{:S(2)}) %copy-start) | copy-done | bytes 2097176
  62.0 0.0 copy-start.1
  62.0 0.9 copy-done.1
  62.9 2.0 %scores.1 = f32[512,128]{1,0:T(8,128)} custom-call(s32[1,512]{1,0:T(1,128)} %bitcast.11, f32[32,5,4,128]{3,2,1,0:T(4,128)S(1)} %all-to-all-done.2.g_ref, f32[8,4,32,4,128]{4,3,2,1,0:T(4,128)S(1)} %copy-done, f32[4,32,4,128]{3,2,1,0:T(4,128)S(1)} %copy-done.1), custom_call_target="tpu_custom_call" | custom-call | tf_op jit(solution)/shard_map/scores/pallas_call | solution.py:204
  64.9 21.1 %all-to-all-start.3 = ((f32[512,1,128]{2,1,0:T(1,128)}), f32[512,1,128]{2,1,0:T(1,128)S(1)}, u32[]{:S(2)}, u32[]{:S(2)}) async-start(f32[512,1,128]{2,1,0:T(1,128)} %bitcast.9), calls=%async_computation.3 | async-start | bytes 524288 | tf_op jit(solution)/shard_map/all_to_all | solution.py:390
  86.0 4.5 %collective-permute-start.1 = (f32[8,29,4,128]{3,2,1,0:T(4,128)S(1)}, f32[8,29,4,128]{3,2,1,0:T(4,128)S(1)}, u32[]{:S(2)}, u32[]{:S(2)}) collective-permute-start(f32[8,29,4,128]{3,2,1,0:T(4,128)S(1)} %slice.3.own_ref), channel_id=1, source_target_pairs={{0,384},{128,0},{256,128},{384,256},{1,385},{129,1},{257,129},{385... | collective-permute-start | bytes 1425416 | tf_op jit(solution)/shard_map/ppermute | solution.py:364
  90.5 0.0 collective-permute-done.left_ref
  90.5 1.9 %collective-permute-start.2 = (f32[8,29,4,128]{3,2,1,0:T(4,128)S(1)}, f32[8,29,4,128]{3,2,1,0:T(4,128)S(1)}, u32[]{:S(2)}, u32[]{:S(2)}) collective-permute-start(f32[8,29,4,128]{3,2,1,0:T(4,128)S(1)} %collective-permute-done.left_ref), channel_id=1, source_target_pairs={{0,128},{128,256},{256,384},{384,0},{1,129},{129,257},{257,385},{3... | collective-permute-start | bytes 1425416 | tf_op jit(solution)/shard_map/ppermute | solution.py:364
  92.4 0.0 copy-done.3
  92.4 1.1 %gram_rows.1.rows_ref = f32[8,4,128]{2,1,0:T(4,128)} custom-call(s32[1]{0:T(128)} %bitcast.1.first_ref, f32[32,5,4,128]{3,2,1,0:T(4,128)S(1)} %all-to-all-done.2.g_ref, f32[5,4,128]{2,1,0:T(4,128)S(1)} %copy-done.3), custom_call_target="tpu_custom_call" | custom-call | tf_op jit(solution)/shard_map/gram_rows/pallas_call | solution.py:239
  93.6 0.0 copy-start.2
  93.6 8.1 %collective-permute-done.1.right_ref = f32[8,29,4,128]{3,2,1,0:T(4,128)S(1)} collective-permute-done((f32[8,29,4,128]{3,2,1,0:T(4,128)S(1)}, f32[8,29,4,128]{3,2,1,0:T(4,128)S(1)}, u32[]{:S(2)}, u32[]{:S(2)}) %collective-permute-start.1) | collective-permute-done | bytes 475168 | tf_op jit(solution)/shard_map/ppermute | solution.py:364
  101.7 4.4 %collective-permute-done.2.far_ref = f32[8,29,4,128]{3,2,1,0:T(4,128)S(1)} collective-permute-done((f32[8,29,4,128]{3,2,1,0:T(4,128)S(1)}, f32[8,29,4,128]{3,2,1,0:T(4,128)S(1)}, u32[]{:S(2)}, u32[]{:S(2)}) %collective-permute-start.2) | collective-permute-done | bytes 475168 | tf_op jit(solution)/shard_map/ppermute | solution.py:364
  106.0 6.4 %quantize.1 = bf16[512,1024]{1,0:T(8,128)(2,1)} custom-call(s32[8]{0:T(128)} %bits_ref.1, s32[1]{0:T(128)} %bitcast.x_ref, bf16[512,1024]{1,0:T(8,128)(2,1)} %w_ref.3, f32[8,29,4,128]{3,2,1,0:T(4,128)S(1)} %slice.3.own_ref, f32[8,29,4,128]{3,2,1,0:T(4,128)S(1)} %collective-permute-done.left_ref, f32[8,29,4,128]{3,2,1,0:T(4,128)S(1)} %collective-permute-done.1.right_ref, ...), custom_call_target="tpu_custom_call" | custom-call | tf_op jit(solution)/shard_map/quantize/pallas_call | solution.py:340
  112.5 0.0 all-to-all-done.3
  112.5 0.0 copy-done.2
  112.5 0.8 finish.1
  (1 shorter events, 0.0 us)
Async XLA Ops:
  3.1 10.7 %all-to-all-start = ((f32[4,8,5,4,128]{4,3,2,1,0:T(4,128)}), f32[4,8,5,4,128]{4,3,2,1,0:T(4,128)S(1)}, u32[]{:S(2)}, u32[]{:S(2)}) async-start(f32[4,8,5,4,128]{4,3,2,1,0:T(4,128)} %gram_partial.1), calls=%async_computation | async-start | bytes 655360 | tf_op jit(solution)/shard_map/all_to_all | solution.py:360
  42.0 18.4 %all-to-all-start.2 = ((f32[32,5,4,128]{3,2,1,0:T(4,128)}), f32[32,5,4,128]{3,2,1,0:T(4,128)S(1)}, u32[]{:S(2)}, u32[]{:S(2)}) async-start(f32[32,5,4,128]{3,2,1,0:T(4,128)} %get-tuple-element.11), calls=%async_computation.2 | async-start | bytes 655360 | tf_op jit(solution)/shard_map/all_to_all | solution.py:360
  46.1 46.3 %copy-start.3 = (f32[5,4,128]{2,1,0:T(4,128)S(1)}, f32[5,4,128]{2,1,0:T(4,128)}, u32[]{:S(2)}) copy-start(f32[5,4,128]{2,1,0:T(4,128)} %get-tuple-element.16.own_ref) | copy-start | bytes 30724
  46.1 44.4 %collective-permute-start = (f32[8,29,4,128]{3,2,1,0:T(4,128)S(1)}, f32[8,29,4,128]{3,2,1,0:T(4,128)S(1)}, u32[]{:S(2)}, u32[]{:S(2)}) collective-permute-start(f32[8,29,4,128]{3,2,1,0:T(4,128)S(1)} %slice.3.own_ref), channel_id=1, source_target_pairs={{0,128},{128,256},{256,384},{384,0},{1,129},{129,257},{257,385},{3... | collective-permute-start | bytes 1425416 | tf_op jit(solution)/shard_map/ppermute | solution.py:364
  60.4 1.6 %copy-start = (f32[8,4,32,4,128]{4,3,2,1,0:T(4,128)S(1)}, f32[8,4,32,4,128]{4,3,2,1,0:T(4,128)}, u32[]{:S(2)}) copy-start(f32[8,4,32,4,128]{4,3,2,1,0:T(4,128)} %get-tuple-element.13.s_ref) | copy-start | bytes 6291460
  62.0 0.9 copy-start.1
  64.9 47.5 %all-to-all-start.3 = ((f32[512,1,128]{2,1,0:T(1,128)}), f32[512,1,128]{2,1,0:T(1,128)S(1)}, u32[]{:S(2)}, u32[]{:S(2)}) async-start(f32[512,1,128]{2,1,0:T(1,128)} %bitcast.9), calls=%async_computation.3 | async-start | bytes 524288 | tf_op jit(solution)/shard_map/all_to_all | solution.py:390
  86.0 15.7 %collective-permute-start.1 = (f32[8,29,4,128]{3,2,1,0:T(4,128)S(1)}, f32[8,29,4,128]{3,2,1,0:T(4,128)S(1)}, u32[]{:S(2)}, u32[]{:S(2)}) collective-permute-start(f32[8,29,4,128]{3,2,1,0:T(4,128)S(1)} %slice.3.own_ref), channel_id=1, source_target_pairs={{0,384},{128,0},{256,128},{384,256},{1,385},{129,1},{257,129},{385... | collective-permute-start | bytes 1425416 | tf_op jit(solution)/shard_map/ppermute | solution.py:364
  90.5 15.5 %collective-permute-start.2 = (f32[8,29,4,128]{3,2,1,0:T(4,128)S(1)}, f32[8,29,4,128]{3,2,1,0:T(4,128)S(1)}, u32[]{:S(2)}, u32[]{:S(2)}) collective-permute-start(f32[8,29,4,128]{3,2,1,0:T(4,128)S(1)} %collective-permute-done.left_ref), channel_id=1, source_target_pairs={{0,128},{128,256},{256,384},{384,0},{1,129},{129,257},{257,385},{3... | collective-permute-start | bytes 1425416 | tf_op jit(solution)/shard_map/ppermute | solution.py:364
  93.6 18.9 %copy-start.2 = (f32[8,4,128]{2,1,0:T(4,128)S(1)}, f32[8,4,128]{2,1,0:T(4,128)}, u32[]{:S(2)}) copy-start(f32[8,4,128]{2,1,0:T(4,128)} %gram_rows.1.rows_ref) | copy-start | bytes 49156
